TPU v7x, 32 devices: a whole 2x2x4 slice. The times are simulated.
32 devices in a mesh: grp: 8 (over y, x, core), pos: 4 (over z).
Axes of the slice: x: 2, y: 2, z: 4, core: 2. Of those that a mesh axis runs over, the one named last changes fastest.
Arguments:
- hidden_in: bfloat16 [16384, 768], P(('grp', 'pos')), may hold values from -6 to 6
- ln1_gain: bfloat16 [768], replicated, may hold values from 0.099609375 to 1.8984375
- ln1_shift: bfloat16 [768], replicated, may hold values from -1.75 to 1.75
- w_qkv: bfloat16 [768, 2304], replicated, may hold values from -0.21875 to 0.21875
- b_query: bfloat16 [768], replicated, may hold values from -3 to 3
- b_value: bfloat16 [768], replicated, may hold values from -1.75 to 1.75
- w_out: bfloat16 [768, 768], replicated, may hold values from -1.75 to 1.75
- b_out: bfloat16 [768], replicated, may hold values from -1.75 to 1.75
- ln2_gain: bfloat16 [768], replicated, may hold values from 0.099609375 to 1.8984375
- ln2_shift: bfloat16 [768], replicated, may hold values from -1.75 to 1.75
- w_up: bfloat16 [768, 3072], replicated, may hold values from -0.21875 to 0.21875
- b_up: bfloat16 [3072], replicated, may hold values from -1.75 to 1.75
- w_down: bfloat16 [3072, 768], replicated, may hold values from -0.109375 to 0.109375
- b_down: bfloat16 [768], replicated, may hold values from -1.75 to 1.75
- cotangent: bfloat16 [16384, 768], P(('grp', 'pos')), may hold values from -6 to 6
- sol_count: int32 [8], P('grp'), may hold values from 4 to 16, as said below
- prefix_len: int32 [8], P('grp'), may hold values from 128 to 512
- sol_len: int32 [8, 16], P('grp'), may hold values from 48 to 96, as said below
Outputs:
- layer_out: bfloat16 [16384, 768], P(('grp', 'pos'))
- input_grad: bfloat16 [16384, 768], P(('grp', 'pos'))
- grad_ln1_gain: float32 [768], replicated
- grad_ln1_shift: float32 [768], replicated
- grad_w_qkv: float32 [768, 2304], replicated
- grad_b_query: float32 [768], replicated
- grad_b_value: float32 [768], replicated
- grad_w_out: float32 [768, 768], replicated
- grad_b_out: float32 [768], replicated
- grad_ln2_gain: float32 [768], replicated
- grad_ln2_shift: float32 [768], replicated
- grad_w_up: float32 [768, 3072], replicated
- grad_b_up: float32 [3072], replicated
- grad_w_down: float32 [3072, 768], replicated
- grad_b_down: float32 [768], replicated
Inputs may be any that keep to these rules, and one draw needn't show every extreme that they name: `sol_count`: each group has at least 4 solutions; the largest count is reached in every draw. `sol_len`: slots j with j >= sol_count of their group are unused; the lengths of a group never exceed 2048 in sum.
All inputs are finite; a program needn't handle non-finite values.
Results may differ from a plain program's by a relative error of at most 0.012.
Values may be sent and summed in bfloat16 or wider, within the bound.
No kernel may reach another device: no remote copies, remote signals or barrier semaphores. Data moves between devices by JAX's collectives and lax.ppermute only.
A program may use at most 256 MiB of HBM per device.

v0:
```python
import jax
import jax.numpy as jnp
from jax import lax
from jax.sharding import PartitionSpec as P

HD = 64


eps_norm = 1e-05
neg_fill = -1e30


def norm_rows(values, norm_gain, norm_shift):
    average = jnp.mean(values, axis=-1, keepdims=True)
    centred = values - average
    spread = jnp.mean(centred * centred, axis=-1, keepdims=True)
    return centred * lax.rsqrt(spread + eps_norm) * norm_gain + norm_shift


def gelu_tanh(values):
    return jax.nn.gelu(values, approximate=True)


def outer_rows(first_op, second_op):
    return lax.dot_general(
        first_op, second_op, (((0,), (0,)), ((), ())), preferred_element_type=jnp.float32
    )


def times_back(gradient, weight):
    return lax.dot_general(
        gradient, weight, (((1,), (1,)), ((), ())), preferred_element_type=jnp.float32
    )


def column_sum(gradient):
    return jnp.sum(gradient.astype(jnp.float32), axis=0)


def segment_of(positions, sol_total, prefix, sol_lens):
    slot_ids = jnp.arange(sol_lens.shape[0], dtype=jnp.int32)
    lengths = jnp.concatenate([prefix.reshape(1), jnp.where(slot_ids < sol_total, sol_lens, 0)])
    seg_ends = jnp.cumsum(lengths)
    seg_starts = seg_ends - lengths
    segment = jnp.sum((seg_starts[None, :] <= positions[:, None]).astype(jnp.int32), axis=1) - 1
    return (segment, positions < seg_ends[-1])


def allowed_mask(query_pos, key_pos, sol_total, prefix, sol_lens):
    query_seg, query_real = segment_of(query_pos, sol_total, prefix, sol_lens)
    key_seg, key_real = segment_of(key_pos, sol_total, prefix, sol_lens)
    shared = (key_seg[None, :] == 0) | (key_seg[None, :] == query_seg[:, None])
    causal = key_pos[None, :] <= query_pos[:, None]
    inside = query_real[:, None] & key_real[None, :] & causal & shared
    return inside | (key_pos[None, :] == query_pos[:, None])


def body(
    hidden_in,
    ln1_gain,
    ln1_shift,
    w_qkv,
    b_query,
    b_value,
    w_out,
    b_out,
    ln2_gain,
    ln2_shift,
    w_up,
    b_up,
    w_down,
    b_down,
    cotangent,
    sol_count,
    prefix_len,
    sol_len,
):
    row_count = hidden_in.shape[0]
    width = hidden_in.shape[1]
    set_length = row_count * lax.axis_size("pos")
    blocks = width // 128
    per_block = 128 // HD
    scale = HD ** (-0.5)
    query_pos = lax.axis_index("pos") * row_count + jnp.arange(row_count, dtype=jnp.int32)
    key_pos = jnp.arange(set_length, dtype=jnp.int32)
    allowed = allowed_mask(query_pos, key_pos, sol_count[0], prefix_len[0], sol_len[0])

    def to_blocks(matrix):
        return matrix.reshape(matrix.shape[0], blocks, 128).transpose(1, 0, 2)

    def from_blocks(stacked):
        return stacked.transpose(1, 0, 2).reshape(stacked.shape[1], width)

    def block_scores(query_blk, key_blk):
        heads_q = query_blk.reshape(row_count, per_block, HD)
        heads_k = key_blk.reshape(set_length, per_block, HD)
        raw = (
            jnp.einsum("qhd,khd->hqk", heads_q, heads_k, preferred_element_type=jnp.float32) * scale
        )
        return jnp.where(allowed[None], raw, neg_fill)

    def attend(operands):
        query_blk, key_blk, value_blk = operands
        scores = block_scores(query_blk, key_blk)
        row_max = jnp.max(scores, axis=-1, keepdims=True)
        expo = jnp.exp(scores - row_max)
        row_total = jnp.sum(expo, axis=-1, keepdims=True)
        probs = (expo / row_total).astype(jnp.bfloat16)
        heads_v = value_blk.reshape(set_length, per_block, HD)
        output = jnp.einsum("hqk,khd->qhd", probs, heads_v, preferred_element_type=jnp.float32)
        return (output.reshape(row_count, 128), row_max[..., 0] + jnp.log(row_total[..., 0]))

    def attend_back(operands):
        query_blk, key_blk, value_blk, grad_blk, logsum_blk = operands
        scores = block_scores(query_blk, key_blk)
        probs = jnp.exp(scores - logsum_blk[..., None])
        heads_q = query_blk.reshape(row_count, per_block, HD)
        heads_k = key_blk.reshape(set_length, per_block, HD)
        heads_v = value_blk.reshape(set_length, per_block, HD)
        heads_g = grad_blk.reshape(row_count, per_block, HD)
        grad_probs = jnp.einsum(
            "qhd,khd->hqk", heads_g, heads_v, preferred_element_type=jnp.float32
        )
        inner = jnp.sum(grad_probs * probs, axis=-1, keepdims=True)
        grad_scores = (probs * (grad_probs - inner)).astype(jnp.bfloat16)
        grad_q = (
            jnp.einsum("hqk,khd->qhd", grad_scores, heads_k, preferred_element_type=jnp.float32)
            * scale
        )
        grad_k = (
            jnp.einsum("hqk,qhd->khd", grad_scores, heads_q, preferred_element_type=jnp.float32)
            * scale
        )
        grad_v = jnp.einsum(
            "hqk,qhd->khd", probs.astype(jnp.bfloat16), heads_g, preferred_element_type=jnp.float32
        )
        return (
            grad_q.reshape(row_count, 128),
            grad_k.reshape(set_length, 128),
            grad_v.reshape(set_length, 128),
        )

    inputs = hidden_in.astype(jnp.float32)
    normed1, norm1_pull = jax.vjp(
        norm_rows, inputs, ln1_gain.astype(jnp.float32), ln1_shift.astype(jnp.float32)
    )
    normed1_low = normed1.astype(jnp.bfloat16)
    qkv = jnp.dot(normed1_low, w_qkv, preferred_element_type=jnp.float32)
    query = (qkv[:, :width] + b_query.astype(jnp.float32)).astype(jnp.bfloat16)
    key_here = qkv[:, width : 2 * width].astype(jnp.bfloat16)
    value_here = (qkv[:, 2 * width :] + b_value.astype(jnp.float32)).astype(jnp.bfloat16)
    key_all, value_all = (
        lax.all_gather(key_here, "pos", axis=0, tiled=True),
        lax.all_gather(value_here, "pos", axis=0, tiled=True),
    )
    stacked_out, logsum = lax.map(
        attend, (to_blocks(query), to_blocks(key_all), to_blocks(value_all))
    )
    attended = from_blocks(stacked_out).astype(jnp.bfloat16)
    branch = jnp.dot(attended, w_out, preferred_element_type=jnp.float32) + b_out.astype(
        jnp.float32
    )
    middle = inputs + branch
    normed2, norm2_pull = jax.vjp(
        norm_rows, middle, ln2_gain.astype(jnp.float32), ln2_shift.astype(jnp.float32)
    )
    normed2_low = normed2.astype(jnp.bfloat16)
    pre_act = jnp.dot(normed2_low, w_up, preferred_element_type=jnp.float32) + b_up.astype(
        jnp.float32
    )
    activ, gelu_pull = jax.vjp(gelu_tanh, pre_act)
    activ_low = activ.astype(jnp.bfloat16)
    result = (
        middle
        + jnp.dot(activ_low, w_down, preferred_element_type=jnp.float32)
        + b_down.astype(jnp.float32)
    )
    upstream = cotangent.astype(jnp.float32)
    grad_w_down = outer_rows(activ_low, cotangent)
    grad_b_down = column_sum(cotangent)
    grad_activ = times_back(cotangent, w_down)
    grad_pre = gelu_pull(grad_activ)[0].astype(jnp.bfloat16)
    grad_w_up = outer_rows(normed2_low, grad_pre)
    grad_b_up = column_sum(grad_pre)
    grad_normed2 = times_back(grad_pre, w_up)
    grad_mid_part, grad_ln2_gain, grad_ln2_shift = norm2_pull(grad_normed2)
    grad_middle = upstream + grad_mid_part
    grad_branch = grad_middle.astype(jnp.bfloat16)
    grad_w_out = outer_rows(attended, grad_branch)
    grad_b_out = column_sum(grad_branch)
    grad_attended = times_back(grad_branch, w_out).astype(jnp.bfloat16)
    stacked_q, stacked_k, stacked_v = lax.map(
        attend_back,
        (
            to_blocks(query),
            to_blocks(key_all),
            to_blocks(value_all),
            to_blocks(grad_attended),
            logsum,
        ),
    )
    grad_query = from_blocks(stacked_q).astype(jnp.bfloat16)
    key_terms = from_blocks(stacked_k)
    value_terms = from_blocks(stacked_v)
    key_grad, value_grad = (
        lax.psum_scatter(key_terms, "pos", scatter_dimension=0, tiled=True),
        lax.psum_scatter(value_terms, "pos", scatter_dimension=0, tiled=True),
    )
    grad_value = value_grad.astype(jnp.bfloat16)
    grad_qkv = jnp.concatenate([grad_query, key_grad.astype(jnp.bfloat16), grad_value], axis=1)
    grad_w_qkv = outer_rows(normed1_low, grad_qkv)
    grad_b_query = column_sum(grad_query)
    grad_b_value = column_sum(grad_value)
    grad_normed1 = times_back(grad_qkv, w_qkv)
    grad_in_part, grad_ln1_gain, grad_ln1_shift = norm1_pull(grad_normed1)
    input_grad = (grad_middle + grad_in_part).astype(jnp.bfloat16)
    summed = lax.psum(
        (
            grad_ln1_gain,
            grad_ln1_shift,
            grad_w_qkv,
            grad_b_query,
            grad_b_value,
            grad_w_out,
            grad_b_out,
            grad_ln2_gain,
            grad_ln2_shift,
            grad_w_up,
            grad_b_up,
            grad_w_down,
            grad_b_down,
        ),
        ("grp", "pos"),
    )
    return (result.astype(jnp.bfloat16), input_grad) + tuple(summed)


def solution(mesh):
    placed = (
        P(("grp", "pos"), None),
        P(),
        P(),
        P(),
        P(),
        P(),
        P(),
        P(),
        P(),
        P(),
        P(),
        P(),
        P(),
        P(),
        P(("grp", "pos"), None),
        P("grp"),
        P("grp"),
        P("grp", None),
    )
    return jax.shard_map(
        body,
        mesh=mesh,
        in_specs=placed,
        out_specs=(
            P(("grp", "pos"), None),
            P(("grp", "pos"), None),
            P(),
            P(),
            P(),
            P(),
            P(),
            P(),
            P(),
            P(),
            P(),
            P(),
            P(),
            P(),
            P(),
        ),
        check_vma=False,
    )
```

profile of v0, /device:TPU:0, one launch (start us, length us, event | category | flops | bytes accessed | tf_op | source)
XLA Modules:
  0.0 1088.3 jit_solution(6447770168201648372)
XLA Ops:
  13.2 3.3 fusion.50
  37.6 48.8 %all-gather.3.cloned.1.call-done = bf16[2048,768]{1,0:T(8,128)(2,1)} async-done(((bf16[512,768]{1,0:T(8,128)(2,1)}), bf16[2048,768]{1,0:T(8,128)(2,1)}) %all-gather.3.cloned.1.call-update) | async-done | bytes 3145744 | tf_op jit(solution)/shard_map/all_gather | solution.py:154
  86.5 4.6 copy.43
  91.1 59.6 %all-gather.5.cloned.1.call-done = bf16[2048,768]{1,0:T(8,128)(2,1)} async-done(((bf16[512,768]{1,0:T(8,128)(2,1)}), bf16[2048,768]{1,0:T(8,128)(2,1)}) %all-gather.5.cloned.1.call-update) | async-done | bytes 3145744 | tf_op jit(solution)/shard_map/all_gather | solution.py:153
  150.7 4.6 copy.45
  156.3 85.0 %while.28 = (s32[]{:T(128)}, bf16[6,512,128]{1,2,0:T(8,128)(2,1)}, f32[6,2,512]{2,1,0:T(2,128)}, bf16[6,2048,128]{1,2,0:T(8,128)(2,1)}, bf16[6,512,128]{1,2,0:T(...) while((s32[]{:T(128)}, bf16[6,512,128]{1,2,0:T(8,128)(2,1)}, ...), condition=%wide.region_8.9_spmd.clone, body=%wide.region_5.8_spmd.clone.sunk | while | flops 570424320 | bytes 33342100 | solution.py:156
  157.6 3.6 fusion.114
  171.8 3.6 fusion.114
  185.9 3.6 fusion.114
  200.1 3.6 fusion.114
  214.3 3.6 fusion.114
  228.4 3.6 fusion.114
  244.6 4.9 fusion.54
  249.6 7.2 convert_reduce_fusion
  256.8 3.5 multiply_reduce_fusion.1
  269.0 127.9 %while.29 = (s32[]{:T(128)}, bf16[6,512,128]{1,2,0:T(8,128)(2,1)}, f32[6,2048,128]{1,2,0:T(8,128)}, f32[6,2048,128]{1,2,0:T(8,128)}, bf16[6,2048,128]{1,2,0:T(8,...) while((s32[]{:T(128)}, bf16[6,512,128]{1,2,0:T(8,128)(2,1)}, ...), condition=%wide.region_15.16_spmd.clone, body=%wide.region_13.15_spmd.clone.sunk | while | flops 1382415360 | bytes 78576392 | solution.py:192
  320.6 3.0 multiply_reduce_fusion.5
  341.9 3.0 multiply_reduce_fusion.5
  363.2 3.0 multiply_reduce_fusion.5
  384.5 3.0 multiply_reduce_fusion.5
  397.8 3.6 fusion.62
  401.4 9.8 fusion.53
  411.2 10.2 fusion.55
  421.4 85.2 %reduce-scatter.5.cloned.1.call-done = f32[512,768]{0,1:T(8,128)} async-done(((f32[2048,768]{0,1:T(8,128)}), f32[512,768]{0,1:T(8,128)}) %reduce-scatter.5.cloned.1.call-update) | async-done | bytes 1572880 | tf_op jit(solution)/shard_map/reduce_scatter | solution.py:207
  509.5 111.1 %reduce-scatter.3.cloned.1.call-done = f32[512,768]{0,1:T(8,128)} async-done(((f32[2048,768]{0,1:T(8,128)}), f32[512,768]{0,1:T(8,128)}) %reduce-scatter.3.cloned.1.call-update) | async-done | bytes 1572880 | tf_op jit(solution)/shard_map/reduce_scatter | solution.py:206
  623.0 6.9 fusion.42
  632.5 10.9 %add_convert_fusion.1 = bf16[512,768]{1,0:T(8,128)(2,1)} fusion(f32[512,768]{1,0:T(8,128)} %copy-done.4, bf16[3072,768]{1,0:T(8,128)(2,1)} %param.34, f32[768]{0:T(1024)S(1)} %convert_element_type.139, f32[512,3072]{1,0:T(8,128)} %copy-done.45, f32[3072]{0:T(1024)} %convert_element_type.137), kind=kOutput, calls=%fused_computation.84 | convolution fusion | flops 2432827392 | bytes 13384704 | tf_op jit(solution)/shard_map/dot_general | solution.py:175
  649.9 44.5 %all-reduce = (f32[768]{0:T(1024)}, f32[768]{0:T(1024)}, f32[768]{0:T(1024)}, f32[768]{0:T(1024)}, f32[768]{0:T(1024)}, /*index=5*/f32[768]{0:T(1024)}, f32[768]{0:T(1024)}, f32[3072]{0:T(1024)}, f32[768]{0:T(1024)}) all-reduce(f32[768]{0:T(1024)} %get-tuple-element.184, ...), channel_id=1, replica_groups=mesh['grp'=8,'pos'=4] {'grp','pos'}, use_global_device_ids=true, to_apply=%region_21.22 | all-reduce | flops 9216 | bytes 73728 | tf_op jit(solution)/shard_map/psum | solution.py:217
  694.4 366.1 %all-reduce.4.cloned.1.call-done = (f32[768,2304]{1,0:T(8,128)}, f32[768,768]{1,0:T(8,128)}, f32[768,3072]{1,0:T(8,128)}, f32[3072,768]{1,0:T(8,128)}) async-done(((f32[768,2304]{1,0:T(8,128)}, f32[768,768]{1,0:T(8,128)}, f32[768,3072]{1,0:T(8,128)}, f32[3072,768]{1,0:T(8,128)}), (f32[768,2304]{1,0:T(8,128)}, f32[768,768]{1,0:T(8,128)}, f32[768,3072]{1,0:T(8,128)}, ...) | async-done | bytes 28311568 | tf_op jit(solution)/shard_map/psum | solution.py:217
  1060.5 6.6 copy.82
  1068.5 9.3 copy.84
  1077.8 3.7 copy.85
  (328 shorter events, 233.9 us)
Async XLA Ops:
  7.2 6.0 copy-start
  7.2 79.3 %all-gather.3.cloned.1.call-start = ((), (), s32[]{:S(2)}) async-start(), calls=%async_computation.2 | async-start | bytes 3932160 | tf_op jit(solution)/shard_map/all_gather | solution.py:154
  8.1 8.4 copy-start.37
  9.0 7.5 copy-start.18
  10.3 6.2 copy-start.20
  18.7 5.5 copy-start.44
  18.7 8.1 copy-start.41
  20.1 130.6 %all-gather.5.cloned.1.call-start = ((), (), s32[]{:S(2)}) async-start(), calls=%async_computation.3 | async-start | bytes 3932160 | tf_op jit(solution)/shard_map/all_gather | solution.py:153
  22.6 484.0 %reduce-scatter.5.cloned.1.call-start = ((), (), s32[]{:S(2)}) async-start(), calls=%async_computation.5 | async-start | bytes 7864320 | tf_op jit(solution)/shard_map/reduce_scatter | solution.py:207
  241.3 8.2 slice-start.5
  244.2 16.2 %copy-start.4 = (f32[512,768]{1,0:T(8,128)}, f32[512,768]{1,0:T(8,128)S(1)}, u32[]{:S(2)}) copy-start(f32[512,768]{1,0:T(8,128)S(1)} %get-tuple-element.277) | copy-start | bytes 4718596
  244.2 16.2 %copy-start.26 = (f32[512]{0:T(512)}, f32[512]{0:T(512)S(1)}, u32[]{:S(2)}) copy-start(f32[512]{0:T(512)S(1)} %broadcast_multiply_fusion) | copy-start | bytes 6148
  244.5 15.8 %copy-start.35 = (f32[512]{0:T(512)}, f32[512]{0:T(512)S(1)}, u32[]{:S(2)}) copy-start(f32[512]{0:T(512)S(1)} %fusion.45) | copy-start | bytes 6148
  244.6 12.2 %slice-start.3 = ((s8[4718592]{0:T(1024)(128)(4,1)}), s8[4194304]{0:T(1024)(128)(4,1)S(1)}, s32[]{:S(2)}) async-start(s8[4718592]{0:T(1024)(128)(4,1)} %bitcast.163), calls=%async_computation.10 | async-start | bytes 8388608
  249.6 7.2 copy-start.45
  249.6 7.2 slice-start.4
  397.0 223.6 %reduce-scatter.3.cloned.1.call-start = ((), (), s32[]{:S(2)}) async-start(), calls=%async_computation.4 | async-start | bytes 7864320 | tf_op jit(solution)/shard_map/reduce_scatter | solution.py:206
  397.6 662.9 %all-reduce.4.cloned.1.call-start = ((), (), s32[]{:S(2)}) async-start(), calls=%async_computation.6 | async-start | bytes 56623104 | tf_op jit(solution)/shard_map/psum | solution.py:217
  401.4 9.8 copy-start.7
  401.4 9.8 copy-start.34
  421.4 201.6 %copy-start.19 = (f32[768]{0:T(1024)S(1)}, f32[768]{0:T(1024)}, u32[]{:S(2)}) copy-start(f32[768]{0:T(1024)} %copy-done.18) | copy-start | bytes 9220
  421.4 201.6 %copy-start.21 = (f32[512]{0:T(512)S(1)}, f32[512]{0:T(512)}, u32[]{:S(2)}) copy-start(f32[512]{0:T(512)} %copy-done.20) | copy-start | bytes 6148
  421.4 201.6 %copy-start.23 = (f32[512]{0:T(512)S(1)}, f32[512]{0:T(512)}, u32[]{:S(2)}) copy-start(f32[512]{0:T(512)} %copy-done.22) | copy-start | bytes 6148
  421.4 201.6 %copy-start.38 = (f32[768]{0:T(1024)S(1)}, f32[768]{0:T(1024)}, u32[]{:S(2)}) copy-start(f32[768]{0:T(1024)} %copy-done.37) | copy-start | bytes 9220
  632.5 10.9 %copy-start.3 = (bf16[512,768]{1,0:T(8,128)(2,1)S(1)}, bf16[512,768]{1,0:T(8,128)(2,1)}, u32[]{:S(2)}) copy-start(bf16[512,768]{1,0:T(8,128)(2,1)} %param.22) | copy-start | bytes 2359300
  632.5 10.9 %copy-start.9 = (bf16[6,512,128]{1,2,0:T(8,128)(2,1)S(1)}, bf16[6,512,128]{1,2,0:T(8,128)(2,1)}, u32[]{:S(2)}) copy-start(bf16[6,512,128]{1,2,0:T(8,128)(2,1)} %get-tuple-element.109) | copy-start | bytes 2359300
  632.5 10.9 %copy-start.12 = (bf16[512,768]{0,1:T(8,128)(2,1)S(1)}, bf16[512,768]{0,1:T(8,128)(2,1)}, u32[]{:S(2)}) copy-start(bf16[512,768]{0,1:T(8,128)(2,1)} %get-tuple-element.261) | copy-start | bytes 2359300
  632.5 10.9 %copy-start.14 = (bf16[512,768]{0,1:T(8,128)(2,1)S(1)}, bf16[512,768]{0,1:T(8,128)(2,1)}, u32[]{:S(2)}) copy-start(bf16[512,768]{0,1:T(8,128)(2,1)} %copy-done.13) | copy-start | bytes 2359300
  1060.5 6.6 copy-start.11
  1067.1 10.7 slice-start
  1068.5 9.3 slice-start.1
  1068.5 9.3 slice-start.2
  (42 other events, 114.4 us)
Sparse Core Ops, SparseCore 0:
  20.3 66.1 all-gather.2
  88.6 62.0 all-gather.4
  397.1 109.3 reduce-scatter.4
  509.3 111.2 reduce-scatter.2
  630.0 430.4 all-reduce.3
where the time goes:
time: 1090 us
  waiting for transfers between devices  671 us (62%)
  matrix products  149 us (14%)
  local copies, waits for them, and re-layouts  105 us (10%)
  other arithmetic  102 us (9%)
  blocking collectives  44.5 us (4%)
  between operations  15.8 us (1%)
    psum x1, waiting for transfers between devices, body(): lax.psum((grad_ln1_gain, grad_ln1_shift, grad_w_qkv, grad_b_query, grad_b...  366 us
    reduce_scatter x1, waiting for transfers between devices, body(): lax.psum_scatter(key_terms, 'pos', scatter_dimension=0, tiled=True)  111 us
    reduce_scatter x1, waiting for transfers between devices, body(): lax.psum_scatter(value_terms, 'pos', scatter_dimension=0, tiled=True)  85.2 us
    all_gather x1, waiting for transfers between devices, body(): lax.all_gather(key_here, 'pos', axis=0, tiled=True)  59.6 us
    all_gather x1, waiting for transfers between devices, body(): lax.all_gather(value_here, 'pos', axis=0, tiled=True)  48.8 us
    psum x1, blocking collectives, body(): lax.psum((grad_ln1_gain, grad_ln1_shift, grad_w_qkv, grad_b_query, grad_b...  44.5 us
    or x12, other arithmetic, allowed_mask(): return inside | (key_pos[None, :] == query_pos[:, None])  38.3 us
    dynamic_slice x36, local copies, waits for them, and re-layouts, body(): lax.map(attend, (to_blocks(query), to_blocks(key_all), to_blocks(value_al...  37.2 us
  transfers between devices with their start and end apart: 5, of which 5 were waited for; matrix products, arithmetic and copies ran while one was open for 6% of the time, Pallas kernels for 0%

commit v1 on v0

v1 whole, which is shorter than its diff:
```python
import functools

import jax
import jax.numpy as jnp
from jax import lax
from jax.experimental import pallas as pl
from jax.experimental.pallas import tpu as pltpu
from jax.sharding import PartitionSpec as P

HD = 64
BQ = 128
SLABS = 8
PIECES = 4
ROWS = 96
EXTRA = 8

eps_norm = 1e-05
neg_fill = -1e30
f32 = jnp.float32
bf16 = jnp.bfloat16


def dot(a, b, dims):
    return lax.dot_general(a, b, (dims, ((), ())), preferred_element_type=f32)


NN = ((1,), (0,))
NT = ((1,), (1,))
TN = ((0,), (0,))


def norm_stats(values):
    average = jnp.mean(values, axis=-1, keepdims=True)
    centred = values - average
    spread = jnp.mean(centred * centred, axis=-1, keepdims=True)
    inv = lax.rsqrt(spread + eps_norm)
    return centred * inv, inv


def norm_back(grad, gain, xhat, inv):
    e = grad * gain
    return inv * (
        e
        - jnp.mean(e, axis=-1, keepdims=True)
        - xhat * jnp.mean(e * xhat, axis=-1, keepdims=True)
    )


def gelu_tanh(values):
    return jax.nn.gelu(values, approximate=True)


def column_sum(gradient):
    return jnp.sum(gradient.astype(f32), axis=0)


def fill_bias(pos_ref, count_ref, prefix_ref, lens_ref, bias_a, bias_b, rows, reach, tail):
    first = pos_ref[0] * rows
    blocks = rows // BQ
    qpos = first + lax.broadcasted_iota(jnp.int32, (8, rows), 1)
    prefix = prefix_ref[0]
    start = prefix
    seg_start = jnp.where(qpos >= start, start, 0)
    for j in range(lens_ref.shape[1]):
        start = start + jnp.where(j < count_ref[0], lens_ref[0, j], 0)
        seg_start = jnp.where(qpos >= start, start, seg_start)
    real = qpos < start
    seg_start = jnp.where(real, seg_start, qpos)[:1]
    low = jnp.where(real, prefix, 0)[:1]
    qpos = qpos[:1]
    for b in range(blocks):
        at = slice(BQ * b, BQ * b + BQ)
        kpos = lax.broadcasted_iota(jnp.int32, (reach, BQ), 0)
        ok = (kpos <= qpos[:, at]) & ((kpos < low[:, at]) | (kpos >= seg_start[:, at]))
        bias_a[b] = jnp.where(ok, 0.0, neg_fill)
        kpos = first + BQ * b - tail + lax.broadcasted_iota(jnp.int32, (tail + BQ, BQ), 0)
        ok = (kpos <= qpos[:, at]) & (kpos >= seg_start[:, at]) & (kpos >= reach)
        bias_b[b] = jnp.where(ok, 0.0, neg_fill)


def transposed(x):
    return x.astype(f32).T.astype(bf16)


def head_part(x, h):
    lane = lax.broadcasted_iota(jnp.int32, x.shape, 1)
    return jnp.where((lane >= h * HD) & (lane < (h + 1) * HD), x, jnp.zeros_like(x))


def attend_kernel(
    pos_ref, count_ref, prefix_ref, lens_ref,
    q_ref, k_ref, v_ref, kx_ref, vx_ref,
    out_ref, lse_ref,
    bias_a, bias_b, k_ext, v_ext_t, v0_t,
    *, rows, reach, tail,
):
    @pl.when(pl.program_id(0) == 0)
    def _():
        fill_bias(pos_ref, count_ref, prefix_ref, lens_ref, bias_a, bias_b, rows, reach, tail)

    blocks = rows // BQ
    k_ext[:tail] = kx_ref[:tail]
    k_ext[tail:] = k_ref[...]
    v_ext_t[:, :tail] = transposed(vx_ref[:tail])
    v_ext_t[:, tail:] = transposed(v_ref[...])
    v0_t[...] = transposed(vx_ref[tail:])
    k0 = kx_ref[tail:]
    for b in range(blocks):
        query = q_ref[BQ * b : BQ * b + BQ, :] * jnp.asarray(HD**-0.5, bf16)
        k_band = k_ext[BQ * b : BQ * b + BQ + tail, :]
        outs = []
        for h in range(2):
            part = head_part(query, h)
            s_a = dot(k0, part, NT) + bias_a[b]
            s_b = dot(k_band, part, NT) + bias_b[b]
            top = jnp.maximum(
                jnp.max(s_a, axis=0, keepdims=True), jnp.max(s_b, axis=0, keepdims=True)
            )
            p_a = jnp.exp(s_a - top)
            p_b = jnp.exp(s_b - top)
            total = jnp.sum(p_a, axis=0, keepdims=True) + jnp.sum(p_b, axis=0, keepdims=True)
            hs = slice(h * HD, h * HD + HD)
            o = dot(v0_t[hs, :], p_a.astype(bf16), NN) + dot(
                v_ext_t[hs, BQ * b : BQ * b + BQ + tail], p_b.astype(bf16), NN
            )
            outs.append(o * (1.0 / total))
            lse_ref[0, b, h : h + 1, :] = top + jnp.log(total)
        out_ref[BQ * b : BQ * b + BQ, :] = jnp.concatenate(outs, axis=0).T.astype(bf16)


def attend_back_kernel(
    pos_ref, count_ref, prefix_ref, lens_ref,
    q_ref, k_ref, v_ref, kx_ref, vx_ref, g_ref, lse_ref,
    dq_ref, dk_ref, dv_ref, dkx_ref, dvx_ref,
    bias_a, bias_b, k_ext, v_ext, k_ext_t, k0_t, dk_ext, dv_ext, dk0, dv0,
    *, rows, reach, tail,
):
    @pl.when(pl.program_id(0) == 0)
    def _():
        fill_bias(pos_ref, count_ref, prefix_ref, lens_ref, bias_a, bias_b, rows, reach, tail)

    blocks = rows // BQ
    k_ext[:tail] = kx_ref[:tail]
    k_ext[tail:] = k_ref[...]
    v_ext[:tail] = vx_ref[:tail]
    v_ext[tail:] = v_ref[...]
    k_ext_t[:, :tail] = transposed(kx_ref[:tail])
    k_ext_t[:, tail:] = transposed(k_ref[...])
    k0_t[...] = transposed(kx_ref[tail:])
    k0 = kx_ref[tail:]
    v0 = vx_ref[tail:]
    dk_ext[...] = jnp.zeros_like(dk_ext)
    dv_ext[...] = jnp.zeros_like(dv_ext)
    scale = HD**-0.5
    for b in range(blocks):
        at = slice(BQ * b, BQ * b + BQ)
        band = slice(BQ * b, BQ * b + BQ + tail)
        query = q_ref[at, :] * jnp.asarray(scale, bf16)
        grad = g_ref[at, :]
        k_band = k_ext[band, :]
        v_band = v_ext[band, :]
        outs = []
        for h in range(2):
            hs = slice(h * HD, h * HD + HD)
            part = head_part(query, h)
            gpart = head_part(grad, h)
            lse = lse_ref[0, b, h : h + 1, :]
            p_a = jnp.exp(dot(k0, part, NT) + bias_a[b] - lse)
            p_b = jnp.exp(dot(k_band, part, NT) + bias_b[b] - lse)
            dp_a = dot(v0, gpart, NT)
            dp_b = dot(v_band, gpart, NT)
            inner = jnp.sum(p_a * dp_a, axis=0, keepdims=True) + jnp.sum(
                p_b * dp_b, axis=0, keepdims=True
            )
            ds_a = (p_a * (dp_a - inner)).astype(bf16)
            ds_b = (p_b * (dp_b - inner)).astype(bf16)
            dv_a = dot(p_a.astype(bf16), gpart, NN)
            dk_a = dot(ds_a, part, NN)
            if b == 0 and h == 0:
                dv0[...] = dv_a
                dk0[...] = dk_a
            else:
                dv0[...] += dv_a
                dk0[...] += dk_a
            dv_ext[band, :] += dot(p_b.astype(bf16), gpart, NN)
            dk_ext[band, :] += dot(ds_b, part, NN)
            outs.append(dot(k0_t[hs, :], ds_a, NN) + dot(k_ext_t[hs, band], ds_b, NN))
        dq_ref[at, :] = (jnp.concatenate(outs, axis=0) * scale).T.astype(bf16)
    dkx_ref[:tail] = dk_ext[:tail].astype(bf16)
    dkx_ref[tail:] = dk0[...].astype(bf16)
    dvx_ref[:tail] = dv_ext[:tail].astype(bf16)
    dvx_ref[tail:] = dv0[...].astype(bf16)
    dk_ref[...] = dk_ext[tail:].astype(bf16)
    dv_ref[...] = dv_ext[tail:].astype(bf16)


def column_block(rows, offset=0):
    return pl.BlockSpec((rows, 128), lambda i, *_: (0, offset + i))


def attend(scalars, qkv, kvx, rows, reach, tail):
    width = qkv.shape[1] // 3
    steps = width // 128
    blocks = rows // BQ
    extra = reach + tail
    return pl.pallas_call(
        functools.partial(attend_kernel, rows=rows, reach=reach, tail=tail),
        grid_spec=pltpu.PrefetchScalarGridSpec(
            num_scalar_prefetch=4,
            grid=(steps,),
            in_specs=[
                column_block(rows),
                column_block(rows, steps),
                column_block(rows, 2 * steps),
                column_block(extra),
                column_block(extra, steps),
            ],
            out_specs=[
                column_block(rows),
                pl.BlockSpec((1, blocks, 2, BQ), lambda i, *_: (i, 0, 0, 0)),
            ],
            scratch_shapes=[
                pltpu.VMEM((blocks, reach, BQ), f32),
                pltpu.VMEM((blocks, tail + BQ, BQ), f32),
                pltpu.VMEM((tail + rows, 128), bf16),
                pltpu.VMEM((128, tail + rows), bf16),
                pltpu.VMEM((128, reach), bf16),
            ],
        ),
        out_shape=[
            jax.ShapeDtypeStruct((rows, width), bf16),
            jax.ShapeDtypeStruct((steps, blocks, 2, BQ), f32),
        ],
        name="attend",
    )(*scalars, qkv, qkv, qkv, kvx, kvx)


def attend_back(scalars, qkv, kvx, grad, lse, rows, reach, tail):
    width = qkv.shape[1] // 3
    steps = width // 128
    blocks = rows // BQ
    extra = reach + tail
    return pl.pallas_call(
        functools.partial(attend_back_kernel, rows=rows, reach=reach, tail=tail),
        grid_spec=pltpu.PrefetchScalarGridSpec(
            num_scalar_prefetch=4,
            grid=(steps,),
            in_specs=[
                column_block(rows),
                column_block(rows, steps),
                column_block(rows, 2 * steps),
                column_block(extra),
                column_block(extra, steps),
                column_block(rows),
                pl.BlockSpec((1, blocks, 2, BQ), lambda i, *_: (i, 0, 0, 0)),
            ],
            out_specs=[
                column_block(rows),
                column_block(rows),
                column_block(rows),
                column_block(extra),
                column_block(extra),
            ],
            scratch_shapes=[
                pltpu.VMEM((blocks, reach, BQ), f32),
                pltpu.VMEM((blocks, tail + BQ, BQ), f32),
                pltpu.VMEM((tail + rows, 128), bf16),
                pltpu.VMEM((tail + rows, 128), bf16),
                pltpu.VMEM((128, tail + rows), bf16),
                pltpu.VMEM((128, reach), bf16),
                pltpu.VMEM((tail + rows, 128), f32),
                pltpu.VMEM((tail + rows, 128), f32),
                pltpu.VMEM((reach, 128), f32),
                pltpu.VMEM((reach, 128), f32),
            ],
        ),
        out_shape=[
            jax.ShapeDtypeStruct((rows, width), bf16),
            jax.ShapeDtypeStruct((rows, width), bf16),
            jax.ShapeDtypeStruct((rows, width), bf16),
            jax.ShapeDtypeStruct((extra, width), bf16),
            jax.ShapeDtypeStruct((extra, width), bf16),
        ],
        name="attend_back",
    )(*scalars, qkv, qkv, qkv, kvx, kvx, grad, lse)


def mask_of(side, me):
    return me[1] + side * (me[2] - me[1])


def slab_at(place, me):
    side = (place >> 2) ^ me[0]
    return (side << 2) | ((place & 3) ^ mask_of(side, me))


def place_of(slab, me):
    side = slab >> 2
    return ((side ^ me[0]) << 2) | ((slab & 3) ^ mask_of(side, me))


def slab_rows(result, me_ref, out_ref):
    for c in range(PIECES):
        out_ref[0, c ^ (me_ref[3]), :ROWS, :] = result[ROWS * c : ROWS * c + ROWS].astype(bf16)


def outer_kernel(me_ref, a_ref, b_ref, out_ref):
    slab_rows(dot(a_ref[...], b_ref[...], TN), me_ref, out_ref)


def outer_half(me, a, b, half):
    rows, many = a.shape
    wide = many // SLABS
    return pl.pallas_call(
        outer_kernel,
        grid_spec=pltpu.PrefetchScalarGridSpec(
            num_scalar_prefetch=1,
            grid=(4,),
            in_specs=[
                pl.BlockSpec((rows, wide), lambda r, me: (0, slab_at(r + 4 * half, me))),
                pl.BlockSpec(b.shape, lambda r, me: (0, 0)),
            ],
            out_specs=pl.BlockSpec((1, PIECES, ROWS, b.shape[1]), lambda r, me: (r, 0, 0, 0)),
        ),
        out_shape=jax.ShapeDtypeStruct((4, PIECES, ROWS, b.shape[1]), bf16),
        name="outer",
    )(me, a, b)


def mixed_kernel(
    me_ref, dqkv_ref, n_ref, dkvx_ref, nx_ref, att_ref, gb_ref, small_ref, out_ref, *, half
):
    o = slab_at(pl.program_id(0) + 4 * half, me_ref)

    @pl.when(o < 2)
    def _():
        slab_rows(dot(dqkv_ref[...], n_ref[...], TN), me_ref, out_ref)

    @pl.when((o >= 2) & (o < 6))
    def _():
        slab_rows(
            dot(dqkv_ref[...], n_ref[...], TN) + dot(dkvx_ref[...], nx_ref[...], TN),
            me_ref,
            out_ref,
        )

    @pl.when(o >= 6)
    def _():
        slab_rows(dot(att_ref[...], gb_ref[...], TN), me_ref, out_ref)

    for c in range(PIECES):
        value = small_ref[EXTRA * c : EXTRA * c + EXTRA] if c < 2 else jnp.zeros_like(small_ref[:EXTRA])
        out_ref[0, c ^ (me_ref[3]), ROWS:, :] = jnp.where(o == 0, value, 0.0).astype(bf16)


def mixed_half(me, dqkv, normed, dkvx, normed_x, attended, grad_branch, small, half):
    rows, width = normed.shape
    wide = width // 2

    def slab(r, me):
        return slab_at(r + 4 * half, me)

    whole = lambda x: pl.BlockSpec(x.shape, lambda r, me: (0, 0))
    return pl.pallas_call(
        functools.partial(mixed_kernel, half=half),
        grid_spec=pltpu.PrefetchScalarGridSpec(
            num_scalar_prefetch=1,
            grid=(4,),
            in_specs=[
                pl.BlockSpec((rows, wide), lambda r, me: (0, jnp.minimum(slab(r, me), 5))),
                whole(normed),
                pl.BlockSpec(
                    (dkvx.shape[0], wide), lambda r, me: (0, jnp.clip(slab(r, me) - 2, 0, 3))
                ),
                whole(normed_x),
                pl.BlockSpec((rows, wide), lambda r, me: (0, jnp.maximum(slab(r, me) - 6, 0))),
                whole(grad_branch),
                whole(small),
            ],
            out_specs=pl.BlockSpec(
                (1, PIECES, ROWS + EXTRA, width), lambda r, me: (r, 0, 0, 0)
            ),
        ),
        out_shape=jax.ShapeDtypeStruct((4, PIECES, ROWS + EXTRA, width), bf16),
        name="outer_mixed",
    )(me, dqkv, normed, dkvx, normed_x, attended, grad_branch, small)


def slab_of(me_ref, f_ref, g_ref, o):
    far = (o >> 2) != me_ref[0]
    low = me_ref[3]
    pieces = []
    for c in range(PIECES):
        f = f_ref[0, c ^ low, :ROWS, :].astype(f32)
        g = g_ref[0, c ^ low, :ROWS, :].astype(f32)
        pieces.append(jnp.where(far, g, f))
    return jnp.concatenate(pieces, axis=0)


def spread_kernel(me_ref, f_ref, g_ref, out_ref, *, turned):
    slab = slab_of(me_ref, f_ref, g_ref, pl.program_id(0))
    out_ref[...] = slab.T if turned else slab


def half_specs(rows, width):
    spec = pl.BlockSpec((1, PIECES, rows, width), lambda o, me: (place_of(o, me) & 3, 0, 0, 0))
    return [spec, spec]


def spread(me, near, far, turned):
    width = near.shape[-1]
    wide = PIECES * ROWS
    many = SLABS * wide
    return pl.pallas_call(
        functools.partial(spread_kernel, turned=turned),
        grid_spec=pltpu.PrefetchScalarGridSpec(
            num_scalar_prefetch=1,
            grid=(SLABS,),
            in_specs=half_specs(ROWS, width),
            out_specs=pl.BlockSpec((width, wide), lambda o, me: (0, o))
            if turned
            else pl.BlockSpec((wide, width), lambda o, me: (o, 0)),
        ),
        out_shape=jax.ShapeDtypeStruct((width, many) if turned else (many, width), f32),
        name="spread",
    )(me, near, far)


def mixed_spread_kernel(me_ref, f_ref, g_ref, qkv_ref, out_ref, small_ref):
    o = pl.program_id(0)
    slab = slab_of(me_ref, f_ref, g_ref, o)

    @pl.when(o < 6)
    def _():
        qkv_ref[...] = slab.T

    @pl.when(o >= 6)
    def _():
        out_ref[...] = slab

    @pl.when(o == 0)
    def _():
        far = me_ref[0] != 0
        for c in range(2):
            at = c ^ (me_ref[3])
            f = f_ref[0, at, ROWS:, :].astype(f32)
            g = g_ref[0, at, ROWS:, :].astype(f32)
            small_ref[EXTRA * c : EXTRA * c + EXTRA, :] = jnp.where(far, g, f)


def mixed_spread(me, near, far):
    width = near.shape[-1]
    wide = PIECES * ROWS
    return pl.pallas_call(
        mixed_spread_kernel,
        grid_spec=pltpu.PrefetchScalarGridSpec(
            num_scalar_prefetch=1,
            grid=(SLABS,),
            in_specs=half_specs(ROWS + EXTRA, width),
            out_specs=[
                pl.BlockSpec((width, wide), lambda o, me: (0, jnp.minimum(o, 5))),
                pl.BlockSpec((wide, width), lambda o, me: (jnp.maximum(o - 6, 0), 0)),
                pl.BlockSpec((2 * EXTRA, width), lambda o, me: (0, 0)),
            ],
        ),
        out_shape=[
            jax.ShapeDtypeStruct((width, 3 * width), f32),
            jax.ShapeDtypeStruct((width, width), f32),
            jax.ShapeDtypeStruct((2 * EXTRA, width), f32),
        ],
        name="mixed_spread",
    )(me, near, far)


def grp_pairs(step):
    return [(g, step(g)) for g in range(8)]


ROUTES = (
    ("grp", grp_pairs(lambda g: g ^ 1)),
    ("grp", grp_pairs(lambda g: g ^ (2 if g % 2 == 0 else 4))),
    ("grp", grp_pairs(lambda g: g ^ (4 if g % 2 == 0 else 2))),
    ("pos", [(p, p ^ 1) for p in range(4)]),
    ("pos", [(p, p ^ 2) for p in range(4)]),
)


def hop(value, step):
    axis, pairs = ROUTES[step]
    return lax.ppermute(value, axis, pairs)


def added(a, b):
    return (a.astype(f32) + b.astype(f32)).astype(bf16)


def total_halves(near, far, cube):
    if not cube:
        return lax.psum((near, far), ("grp", "pos"))
    shape = near.shape
    count = shape[0] * shape[1]
    keep = near.reshape((count,) + shape[2:])
    send = far.reshape((count,) + shape[2:])
    for step in range(5):
        got = hop(send, step)
        half = count // 2
        if step < 4:
            send = added(keep[half:], got[half:])
            keep = added(keep[:half], got[:half])
            count = half
        else:
            keep = added(keep, got)
    for step in (4, 3, 2, 1):
        keep = jnp.concatenate([keep, hop(keep, step)], axis=0)
    other = hop(keep, 0)
    return keep.reshape(shape), other.reshape(shape)


def fetch_first(value, blocks, cube):
    if cube and blocks == 1:
        place = lax.axis_index("pos")
        got = lax.ppermute(value, "pos", [(0, 2)])
        here = jnp.where(place == 2, got, value)
        got = lax.ppermute(here, "pos", [(0, 1), (2, 3)])
        return jnp.where(place % 2 == 1, got, here)
    rows = value.shape[0]
    return lax.all_gather(value, "pos", axis=0, tiled=True)[: blocks * rows]


def return_first(partial, blocks, rows, cube):
    place = lax.axis_index("pos")
    if cube and blocks == 1:
        low = partial.astype(bf16)
        here = partial.astype(f32) + lax.ppermute(low, "pos", [(1, 0), (3, 2)]).astype(f32)
        got = lax.ppermute(here.astype(bf16), "pos", [(2, 0)])
        mine = here + got.astype(f32)
    else:
        total = lax.psum(partial.astype(bf16), "pos")
        at = jnp.minimum(place, blocks - 1) * rows
        mine = lax.dynamic_slice_in_dim(total, at, rows, axis=0).astype(f32)
    return jnp.where(place < blocks, mine, 0.0)


def body(
    hidden_in,
    ln1_gain,
    ln1_shift,
    w_qkv,
    b_query,
    b_value,
    w_out,
    b_out,
    ln2_gain,
    ln2_shift,
    w_up,
    b_up,
    w_down,
    b_down,
    cotangent,
    sol_count,
    prefix_len,
    sol_len,
):
    rows, width = hidden_in.shape
    n_pos = lax.axis_size("pos")
    n_grp = lax.axis_size("grp")
    cube = n_grp == 8 and n_pos == 4
    set_length = rows * n_pos
    blocks = -(-(set_length // 4) // rows)
    reach = blocks * rows
    tail = -(-(3 * set_length // 64) // BQ) * BQ

    place = lax.axis_index("pos")
    if cube:
        g = lax.axis_index("grp")
        core, x, y = g & 1, (g >> 1) & 1, (g >> 2) & 1
        me = jnp.stack([core, 2 * x + y, 2 * y + x, 2 * (place & 1) + (place >> 1)])
    else:
        me = jnp.zeros((4,), jnp.int32)
    me = me.astype(jnp.int32)
    scalars = (place.astype(jnp.int32).reshape(1), sol_count, prefix_len, sol_len)

    gain1, shift1 = ln1_gain.astype(f32), ln1_shift.astype(f32)
    gain2, shift2 = ln2_gain.astype(f32), ln2_shift.astype(f32)

    tail_in = lax.ppermute(
        hidden_in[rows - tail :], "pos", [(p, p + 1) for p in range(n_pos - 1)]
    )
    first_in = fetch_first(hidden_in, blocks, cube)

    inputs = hidden_in.astype(f32)
    xhat1, inv1 = norm_stats(inputs)
    normed1 = (xhat1 * gain1 + shift1).astype(bf16)
    bias = jnp.concatenate([b_query.astype(f32), jnp.zeros((width,), f32), b_value.astype(f32)])
    qkv = (dot(normed1, w_qkv, NN) + bias).astype(bf16)

    inputs_x = jnp.concatenate([tail_in, first_in], axis=0).astype(f32)
    xhat1_x, _ = norm_stats(inputs_x)
    normed1_x = (xhat1_x * gain1 + shift1).astype(bf16)
    kvx = (dot(normed1_x, w_qkv[:, width:], NN) + bias[width:]).astype(bf16)

    attended, lse = attend(scalars, qkv, kvx, rows, reach, tail)

    middle = inputs + dot(attended, w_out, NN) + b_out.astype(f32)
    xhat2, inv2 = norm_stats(middle)
    normed2 = (xhat2 * gain2 + shift2).astype(bf16)
    pre_act = dot(normed2, w_up, NN) + b_up.astype(f32)
    activ, gelu_pull = jax.vjp(gelu_tanh, pre_act)
    activ = activ.astype(bf16)

    down_far = outer_half(me, activ, cotangent, 1)
    down_near = outer_half(me, activ, cotangent, 0)
    down = total_halves(down_near, down_far, cube)

    grad_activ = dot(cotangent, w_down, NT)
    grad_pre = gelu_pull(grad_activ)[0].astype(bf16)

    up_far = outer_half(me, grad_pre, normed2, 1)
    up_near = outer_half(me, grad_pre, normed2, 0)
    up = total_halves(up_near, up_far, cube)

    grad_normed2 = dot(grad_pre, w_up, NT)
    grad_middle = cotangent.astype(f32) + norm_back(grad_normed2, gain2, xhat2, inv2)
    grad_branch = grad_middle.astype(bf16)
    grad_attended = dot(grad_branch, w_out, NT).astype(bf16)
    dq, dk, dv, dkx, dvx = attend_back(
        scalars, qkv, kvx, grad_attended, lse, rows, reach, tail
    )
    dqkv = jnp.concatenate([dq, dk, dv], axis=1)
    dkvx = jnp.concatenate([dkx, dvx], axis=1)
    grad_normed1 = dot(dqkv, w_qkv, NT)
    grad_normed1_x = dot(dkvx, w_qkv[:, width:], NT)

    small = jnp.concatenate(
        [
            column_sum(cotangent),
            column_sum(grad_pre),
            column_sum(grad_normed2 * xhat2),
            column_sum(grad_normed2),
            column_sum(grad_branch),
            column_sum(dq),
            column_sum(dv) + column_sum(dvx),
            column_sum(grad_normed1 * xhat1) + column_sum(grad_normed1_x * xhat1_x),
            column_sum(grad_normed1) + column_sum(grad_normed1_x),
            jnp.zeros((4 * width,), f32),
        ]
    ).reshape(2 * EXTRA, width)
    mixed_args = (me, dqkv, normed1, dkvx, normed1_x, attended, grad_branch, small)
    mixed_far = mixed_half(*mixed_args, 1)
    mixed_near = mixed_half(*mixed_args, 0)
    mixed = total_halves(mixed_near, mixed_far, cube)

    back_tail = lax.ppermute(
        grad_normed1_x[:tail].astype(bf16), "pos", [(p + 1, p) for p in range(n_pos - 1)]
    )
    back_first = return_first(grad_normed1_x[tail:], blocks, rows, cube)
    grad_normed1 = (
        grad_normed1
        + back_first
        + jnp.concatenate([jnp.zeros((rows - tail, width), f32), back_tail.astype(f32)], axis=0)
    )
    input_grad = (grad_middle + norm_back(grad_normed1, gain1, xhat1, inv1)).astype(bf16)

    layer_out = (middle + dot(activ, w_down, NN) + b_down.astype(f32)).astype(bf16)

    grad_w_down = spread(me, *down, False)
    grad_w_up = spread(me, *up, True)
    grad_w_qkv, grad_w_out, vectors = mixed_spread(me, *mixed)
    return (
        layer_out,
        input_grad,
        vectors[10],
        vectors[11],
        grad_w_qkv,
        vectors[8],
        vectors[9],
        grad_w_out,
        vectors[7],
        vectors[5],
        vectors[6],
        grad_w_up,
        vectors[1:5].reshape(-1),
        grad_w_down,
        vectors[0],
    )


def solution(mesh):
    rows = P(("grp", "pos"), None)
    placed = (rows,) + (P(),) * 13 + (rows, P("grp"), P("grp"), P("grp", None))
    return jax.shard_map(
        body,
        mesh=mesh,
        in_specs=placed,
        out_specs=(rows, rows) + (P(),) * 13,
        check_vma=False,
    )
```

time: 1090 us -> 454 us (0.42)
  waiting for transfers between devices: 671 us -> 169 us
  Pallas kernels: 0 us -> 115 us
  matrix products: 149 us -> 38.6 us
  local copies, waits for them, and re-layouts: 105 us -> 35.8 us
  other arithmetic: 102 us -> 36.8 us
  starting transfers between devices: 0.59 us -> 48.7 us
  blocking collectives: 44.5 us -> 0 us
  between operations: 15.8 us -> 3.04 us
    psum x1 -> x0, waiting for transfers between devices: 366 us -> none  [body(): lax.psum((grad_ln1_gain, grad_ln1_shift, grad_w_qkv, grad_b_query, grad_b...]
    reduce_scatter x2 -> x0, waiting for transfers between devices: 196 us -> none  [the longest x1 111 us: body(): lax.psum_scatter(key_terms, 'pos', scatter_dimension=0, tiled=True)]
    ppermute x0 -> x36, waiting for transfers between devices: none -> 169 us  [the longest x30 129 us: hop(): return lax.ppermute(value, axis, pairs)]
    pallas_call x0 -> x11, Pallas kernels: none -> 115 us  [the longest x1 24.6 us: attend_back(): pl.pallas_call(functools.partial(attend_back_kernel, rows=rows, reach=rea...]
    dot_general x54 -> x10, matrix products: 149 us -> 38.6 us  [dot(): return lax.dot_general(a, b, (dims, ((), ())), preferred_element_type=f32)]
    all_gather x2 -> x0, waiting for transfers between devices: 108 us -> none  [the longest x1 59.6 us: body(): lax.all_gather(key_here, 'pos', axis=0, tiled=True)]
    ppermute x0 -> x36, starting transfers between devices: none -> 48.7 us  [the longest x30 35.1 us: hop(): return lax.ppermute(value, axis, pairs)]
    psum x1 -> x0, blocking collectives: 44.5 us -> none  [body(): lax.psum((grad_ln1_gain, grad_ln1_shift, grad_w_qkv, grad_b_query, grad_b...]
  transfers between devices with their start and end apart: 5 -> 36, of which waited for: 5 -> 21; matrix products, arithmetic and copies ran while one was open for 6% -> 14% of each run, Pallas kernels for 0% -> 13%
where the time goes in v1:
time: 454 us; the launch traced here: 447 us
  waiting for transfers between devices  169 us (37%)
  Pallas kernels  115 us (25%)
  starting transfers between devices  48.7 us (11%)
  matrix products  38.6 us (9%)
  other arithmetic  36.8 us (8%)
  local copies, waits for them, and re-layouts  35.8 us (8%)
    ppermute x30, waiting for transfers between devices, hop(): return lax.ppermute(value, axis, pairs)  129 us
    dot_general x10, matrix products, dot(): return lax.dot_general(a, b, (dims, ((), ())), preferred_element_type=f32)  38.6 us
    ppermute x30, starting transfers between devices, hop(): return lax.ppermute(value, axis, pairs)  35.1 us
    pallas_call x1, Pallas kernels, attend_back(): pl.pallas_call(functools.partial(attend_back_kernel, rows=rows, reach=rea...  24.6 us
    pallas_call x4, Pallas kernels, outer_half(): pl.pallas_call(outer_kernel, grid_spec=pltpu.PrefetchScalarGridSpec(num_s...  22.7 us
    pallas_call x2, Pallas kernels, spread(): pl.pallas_call(functools.partial(spread_kernel, turned=turned), grid_spec...  21 us
    unnamed x122, local copies, waits for them, and re-layouts  20.5 us
    pallas_call x1, Pallas kernels, attend(): pl.pallas_call(functools.partial(attend_kernel, rows=rows, reach=reach, t...  20.1 us
  transfers between devices with their start and end apart: 36, of which 21 were waited for; matrix products, arithmetic and copies ran while one was open for 14% of the time, Pallas kernels for 13%

profile of v1, /device:TPU:0, one launch (start us, length us, event | category | flops | bytes accessed | tf_op | source)
XLA Modules:
  0.0 446.9 jit_solution(7734225228538169164)
XLA Ops:
  0.7 6.2 %collective-permute-start.1 = (bf16[512,768]{1,0:T(8,128)(2,1)}, bf16[512,768]{1,0:T(8,128)(2,1)S(1)}, u32[]{:S(2)}, u32[]{:S(2)}) collective-permute-start(bf16[512,768]{1,0:T(8,128)(2,1)} %param.18), channel_id=1, source_target_pairs={{0,2},{4,6},{8,10},{12,14},{16,18},{20,22},{24,26},{28,30}} | collective-permute-start | bytes 2359304 | tf_op jit(solution)/shard_map/ppermute | solution.py:522
  30.5 14.4 %collective-permute-done.2 = bf16[512,768]{1,0:T(8,128)(2,1)S(1)} collective-permute-done((bf16[512,768]{1,0:T(8,128)(2,1)S(1)}, bf16[512,768]{1,0:T(8,128)(2,1)S(1)}, u32[]{:S(2)}, u32[]{:S(2)}) %collective-permute-start.2) | collective-permute-done | bytes 786464 | tf_op jit(solution)/shard_map/ppermute | solution.py:524
  52.2 20.1 %attend.1 = (bf16[512,768]{1,0:T(8,128)(2,1)}, f32[6,4,2,128]{3,2,1,0:T(2,128)}) custom-call(s32[1]{0:T(128)} %bitcast.pos_ref, s32[1]{0:T(128)S(6)} %copy.58.count_ref, s32[1]{0:T(128)S(6)} %copy.59.prefix_ref, s32[1,16]{1,0:T(1,128)} %lens_ref.3, bf16[512,2304]{1,0:T(8,128)(2,1)} %fusion.7.q_ref.k_ref.v_ref, bf16[512,2304]{1,0:T(8,128)(2,1)} %fusion.7.q_ref.k_ref.v_ref, ...), custom_call_target="tpu_custom_call" | custom-call | tf_op jit(solution)/shard_map/attend/pallas_call | solution.py:206
  75.8 4.6 %fusion.50 = f32[512,3072]{1,0:T(8,128)S(1)} fusion(bf16[512,768]{1,0:T(8,128)(2,1)S(1)} %add_convert_fusion.2.b_ref, bf16[768,3072]{1,0:T(8,128)(2,1)} %param.28), kind=kOutput, calls=%fused_computation.167 | convolution fusion | flops 2415919104 | bytes 11796480 | tf_op jit(solution)/shard_map/dot_general | solution.py:24
  80.5 10.1 %convert_reduce_fusion = (f32[3072]{0:T(1024)}, bf16[512,3072]{1,0:T(8,128)(2,1)S(1)}, bf16[512,3072]{1,0:T(8,128)(2,1)}) fusion(f32[512,3072]{1,0:T(8,128)S(1)} %fusion.50, f32[3072]{0:T(1024)S(1)} %copy-done.38, bf16[512,768]{1,0:T(8,128)(2,1)S(1)} %copy-done.15, bf16[3072,768]{1,0:T(8,128)(2,1)} %param.30), kind=kOutput, calls=%fused_computation.9 | convolution fusion | flops 2455237632 | bytes 18112512 | tf_op jit(solution)/shard_map/dot_general | solution.py:24
  99.2 24.6 %attend_back.1 = (bf16[512,768]{1,0:T(8,128)(2,1)}, bf16[512,768]{1,0:T(8,128)(2,1)}, bf16[512,768]{1,0:T(8,128)(2,1)}, bf16[640,768]{1,0:T(8,128)(2,1)}, bf16[640,768]{1,0:T(8,128)(2,1)}) custom-call(s32[1]{0:T(128)} %bitcast.pos_ref, s32[1]{0:T(128)S(6)} %copy.58.count_ref, s32[1]{0:T(128)S(6)} %copy.59.prefix_ref, s32[1,16]{1,0:T(1,128)} %lens_ref.3, ...), custom_call_target="tpu_custom_call" | custom-call | tf_op jit(solution)/shard_map/attend_back/pallas_call | solution.py:243
  125.5 4.8 %fusion.42 = (f32[768]{0:T(1024)}, f32[768]{0:T(1024)}, f32[640,768]{1,0:T(8,128)S(1)}) fusion(f32[640]{0:T(1024)S(1)} %copy-done.32, f32[640]{0:T(1024)S(1)} %broadcast_multiply_fusion, bf16[512,768]{1,0:T(8,128)(2,1)S(1)} %copy-done.8, bf16[128,768]{1,0:T(8,128)(2,1)} %collective-permute-done, ...), kind=kOutput, calls=%fused_computation.160 | convolution fusion | flops 1514371584 | bytes 7285760 | tf_op jit(solution)/shard_map/dot_general | solution.py:24
  135.3 5.8 %outer.7 = bf16[4,4,96,768]{3,2,1,0:T(8,128)(2,1)} custom-call(s32[4]{0:T(128)} %pad_add_fusion.me_ref, bf16[512,3072]{1,0:T(8,128)(2,1)} %get-tuple-element.65.a_ref, bf16[512,768]{1,0:T(8,128)(2,1)} %b_ref.3), custom_call_target="tpu_custom_call" | custom-call | tf_op jit(solution)/shard_map/outer/pallas_call | solution.py:314
  150.8 7.2 %collective-permute-done.3 = bf16[512,768]{1,0:T(8,128)(2,1)} collective-permute-done((bf16[512,768]{1,0:T(8,128)(2,1)}, bf16[512,768]{1,0:T(8,128)(2,1)}, u32[]{:S(2)}, u32[]{:S(2)}) %collective-permute-start.3) | collective-permute-done | bytes 786464 | tf_op jit(solution)/shard_map/ppermute | solution.py:534
  162.9 17.2 %collective-permute-done.4 = bf16[512,768]{1,0:T(8,128)(2,1)S(1)} collective-permute-done((bf16[512,768]{1,0:T(8,128)(2,1)S(1)}, bf16[512,768]{1,0:T(8,128)(2,1)S(1)}, u32[]{:S(2)}, u32[]{:S(2)}) %collective-permute-start.4) | collective-permute-done | bytes 786464 | tf_op jit(solution)/shard_map/ppermute | solution.py:535
  184.6 7.6 %outer_mixed.3 = bf16[4,4,104,768]{3,2,1,0:T(8,128)(2,1)} custom-call(s32[4]{0:T(128)} %pad_add_fusion.me_ref, bf16[512,2304]{1,0:T(8,128)(2,1)} %copy-done.3, bf16[512,768]{1,0:T(8,128)(2,1)} %copy-done.14, bf16[640,1536]{1,0:T(8,128)(2,1)} %copy-done.9, bf16[640,768]{1,0:T(8,128)(2,1)} %copy-done.11, bf16[512,768]{1,0:T(8,128)(2,1)} %get-tuple-element.25.att_ref, ...), custom_call_target="tpu_custom_call" | custom-call | tf_op jit(solution)/shard_map/outer_mixed/pallas_call | solution.py:364
  192.2 5.6 %outer.5 = bf16[4,4,96,768]{3,2,1,0:T(8,128)(2,1)} custom-call(s32[4]{0:T(128)} %pad_add_fusion.me_ref, bf16[512,3072]{1,0:T(8,128)(2,1)} %copy-done.6, bf16[512,768]{1,0:T(8,128)(2,1)} %copy-done.4), custom_call_target="tpu_custom_call" | custom-call | tf_op jit(solution)/shard_map/outer/pallas_call | solution.py:314
  198.3 5.6 %outer.4 = bf16[4,4,96,768]{3,2,1,0:T(8,128)(2,1)} custom-call(s32[4]{0:T(128)} %pad_add_fusion.me_ref, bf16[512,3072]{1,0:T(8,128)(2,1)} %copy-done.6, bf16[512,768]{1,0:T(8,128)(2,1)} %copy-done.4), custom_call_target="tpu_custom_call" | custom-call | tf_op jit(solution)/shard_map/outer/pallas_call | solution.py:314
  204.0 5.6 %outer.6 = bf16[4,4,96,768]{3,2,1,0:T(8,128)(2,1)} custom-call(s32[4]{0:T(128)} %pad_add_fusion.me_ref, bf16[512,3072]{1,0:T(8,128)(2,1)} %get-tuple-element.65.a_ref, bf16[512,768]{1,0:T(8,128)(2,1)} %b_ref.3), custom_call_target="tpu_custom_call" | custom-call | tf_op jit(solution)/shard_map/outer/pallas_call | solution.py:314
  212.8 7.6 %outer_mixed.2 = bf16[4,4,104,768]{3,2,1,0:T(8,128)(2,1)} custom-call(s32[4]{0:T(128)} %pad_add_fusion.me_ref, bf16[512,2304]{1,0:T(8,128)(2,1)} %copy-done.3, bf16[512,768]{1,0:T(8,128)(2,1)} %copy-done.14, bf16[640,1536]{1,0:T(8,128)(2,1)} %copy-done.9, bf16[640,768]{1,0:T(8,128)(2,1)} %copy-done.11, bf16[512,768]{1,0:T(8,128)(2,1)} %get-tuple-element.25.att_ref, ...), custom_call_target="tpu_custom_call" | custom-call | tf_op jit(solution)/shard_map/outer_mixed/pallas_call | solution.py:364
  234.1 7.3 %collective-permute-done.27 = bf16[8,96,768]{2,1,0:T(8,128)(2,1)S(1)} collective-permute-done((bf16[8,96,768]{2,1,0:T(8,128)(2,1)S(1)}, bf16[8,96,768]{2,1,0:T(8,128)(2,1)S(1)}, u32[]{:S(2)}, u32[]{:S(2)}) %collective-permute-start.27) | collective-permute-done | bytes 1179680 | tf_op jit(solution)/shard_map/ppermute | solution.py:490
  243.5 17.9 %collective-permute-done.7 = bf16[8,104,768]{2,1,0:T(8,128)(2,1)S(1)} collective-permute-done((bf16[8,104,768]{2,1,0:T(8,128)(2,1)S(1)}, bf16[8,104,768]{2,1,0:T(8,128)(2,1)S(1)}, u32[]{:S(2)}, u32[]{:S(2)}) %collective-permute-start.7) | collective-permute-done | bytes 1277984 | tf_op jit(solution)/shard_map/ppermute | solution.py:490
  263.6 17.3 %collective-permute-done.17 = bf16[8,96,768]{2,1,0:T(8,128)(2,1)S(1)} collective-permute-done((bf16[8,96,768]{2,1,0:T(8,128)(2,1)S(1)}, bf16[8,96,768]{2,1,0:T(8,128)(2,1)S(1)}, u32[]{:S(2)}, u32[]{:S(2)}) %collective-permute-start.17) | collective-permute-done | bytes 1179680 | tf_op jit(solution)/shard_map/ppermute | solution.py:490
  285.5 5.6 %collective-permute-done.18 = bf16[4,96,768]{2,1,0:T(8,128)(2,1)S(1)} collective-permute-done((bf16[4,96,768]{2,1,0:T(8,128)(2,1)S(1)}, bf16[4,96,768]{2,1,0:T(8,128)(2,1)S(1)}, u32[]{:S(2)}, u32[]{:S(2)}) %collective-permute-start.18) | collective-permute-done | bytes 589856 | tf_op jit(solution)/shard_map/ppermute | solution.py:490
  293.2 11.6 %collective-permute-done.9 = bf16[2,104,768]{2,1,0:T(8,128)(2,1)S(1)} collective-permute-done((bf16[2,104,768]{2,1,0:T(8,128)(2,1)S(1)}, bf16[2,104,768]{2,1,0:T(8,128)(2,1)S(1)}, u32[]{:S(2)}, u32[]{:S(2)}) %collective-permute-start.9) | collective-permute-done | bytes 319520 | tf_op jit(solution)/shard_map/ppermute | solution.py:490
  309.2 8.8 %collective-permute-done.10 = bf16[1,104,768]{2,1,0:T(8,128)(2,1)S(1)} collective-permute-done((bf16[1,104,768]{2,1,0:T(8,128)(2,1)S(1)}, bf16[1,104,768]{2,1,0:T(8,128)(2,1)S(1)}, u32[]{:S(2)}, u32[]{:S(2)}) %collective-permute-start.10) | collective-permute-done | bytes 159776 | tf_op jit(solution)/shard_map/ppermute | solution.py:490
  321.8 6.5 %collective-permute-done.11 = bf16[1,104,768]{2,1,0:T(8,128)(2,1)S(1)} collective-permute-done((bf16[1,104,768]{2,1,0:T(8,128)(2,1)S(1)}, bf16[1,104,768]{2,1,0:T(8,128)(2,1)S(1)}, u32[]{:S(2)}, u32[]{:S(2)}) %collective-permute-start.11) | collective-permute-done | bytes 159776 | tf_op jit(solution)/shard_map/ppermute | solution.py:490
  335.6 6.1 %collective-permute-done.12 = bf16[2,104,768]{2,1,0:T(8,128)(2,1)S(1)} collective-permute-done((bf16[2,104,768]{2,1,0:T(8,128)(2,1)S(1)}, bf16[2,104,768]{2,1,0:T(8,128)(2,1)S(1)}, u32[]{:S(2)}, u32[]{:S(2)}) %collective-permute-start.12) | collective-permute-done | bytes 319520 | tf_op jit(solution)/shard_map/ppermute | solution.py:490
  355.6 7.1 %collective-permute-done.23 = bf16[4,96,768]{2,1,0:T(8,128)(2,1)S(1)} collective-permute-done((bf16[4,96,768]{2,1,0:T(8,128)(2,1)S(1)}, bf16[4,96,768]{2,1,0:T(8,128)(2,1)S(1)}, u32[]{:S(2)}, u32[]{:S(2)}) %collective-permute-start.23) | collective-permute-done | bytes 589856 | tf_op jit(solution)/shard_map/ppermute | solution.py:490
  363.2 12.1 %collective-permute-done.33 = bf16[4,96,768]{2,1,0:T(8,128)(2,1)S(1)} collective-permute-done((bf16[4,96,768]{2,1,0:T(8,128)(2,1)S(1)}, bf16[4,96,768]{2,1,0:T(8,128)(2,1)S(1)}, u32[]{:S(2)}, u32[]{:S(2)}) %collective-permute-start.33) | collective-permute-done | bytes 589856 | tf_op jit(solution)/shard_map/ppermute | solution.py:490
  381.1 5.6 %collective-permute-done.24 = bf16[8,96,768]{2,1,0:T(8,128)(2,1)S(1)} collective-permute-done((bf16[8,96,768]{2,1,0:T(8,128)(2,1)S(1)}, bf16[8,96,768]{2,1,0:T(8,128)(2,1)S(1)}, u32[]{:S(2)}, u32[]{:S(2)}) %collective-permute-start.24) | collective-permute-done | bytes 1179680 | tf_op jit(solution)/shard_map/ppermute | solution.py:490
  386.8 4.7 %collective-permute-start.25 = (bf16[16,96,768]{2,1,0:T(8,128)(2,1)S(1)}, bf16[16,96,768]{2,1,0:T(8,128)(2,1)S(1)}, u32[]{:S(2)}, u32[]{:S(2)}) collective-permute-start(bf16[16,96,768]{2,1,0:T(8,128)(2,1)S(1)} %constant_dynamic-update-slice_fusion.11), channel_id=1, source_target_pairs={{0,4},{4,0},{8,12},{12,8},{16,20},{20,16},{24,28},{28,24},{1,5},{5... | collective-permute-start | bytes 7077896 | tf_op jit(solution)/shard_map/ppermute | solution.py:490
  391.5 7.8 %collective-permute-done.34 = bf16[8,96,768]{2,1,0:T(8,128)(2,1)S(1)} collective-permute-done((bf16[8,96,768]{2,1,0:T(8,128)(2,1)S(1)}, bf16[8,96,768]{2,1,0:T(8,128)(2,1)S(1)}, u32[]{:S(2)}, u32[]{:S(2)}) %collective-permute-start.34) | collective-permute-done | bytes 1179680 | tf_op jit(solution)/shard_map/ppermute | solution.py:490
  400.4 4.4 collective-permute-start.35
  411.2 10.7 %spread.2 = f32[768,3072]{1,0:T(8,128)} custom-call(s32[4]{0:T(128)} %pad_add_fusion.me_ref, bf16[4,4,96,768]{3,2,1,0:T(8,128)(2,1)} %bitcast.52, bf16[4,4,96,768]{3,2,1,0:T(8,128)(2,1)} %bitcast.56), custom_call_target="tpu_custom_call" | custom-call | tf_op jit(solution)/shard_map/spread/pallas_call | solution.py:414
  421.9 10.3 %spread.3 = f32[3072,768]{1,0:T(8,128)} custom-call(s32[4]{0:T(128)} %pad_add_fusion.me_ref, bf16[4,4,96,768]{3,2,1,0:T(8,128)(2,1)} %bitcast.18.f_ref, bf16[4,4,96,768]{3,2,1,0:T(8,128)(2,1)} %bitcast.19.g_ref), custom_call_target="tpu_custom_call" | custom-call | tf_op jit(solution)/shard_map/spread/pallas_call | solution.py:414
  432.2 11.6 %mixed_spread.1 = (f32[768,2304]{1,0:T(8,128)}, f32[768,768]{1,0:T(8,128)}, f32[16,768]{1,0:T(8,128)}) custom-call(s32[4]{0:T(128)} %pad_add_fusion.me_ref, bf16[4,4,104,768]{3,2,1,0:T(8,128)(2,1)} %bitcast.8.f_ref, bf16[4,4,104,768]{3,2,1,0:T(8,128)(2,1)} %bitcast.9.g_ref), custom_call_target="tpu_custom_call" | custom-call | tf_op jit(solution)/shard_map/mixed_spread/pallas_call | solution.py:454
  (268 shorter events, 141.4 us)
Async XLA Ops:
  0.7 24.4 %collective-permute-start.1 = (bf16[512,768]{1,0:T(8,128)(2,1)}, bf16[512,768]{1,0:T(8,128)(2,1)S(1)}, u32[]{:S(2)}, u32[]{:S(2)}) collective-permute-start(bf16[512,768]{1,0:T(8,128)(2,1)} %param.18), channel_id=1, source_target_pairs={{0,2},{4,6},{8,10},{12,14},{16,18},{20,22},{24,26},{28,30}} | collective-permute-start | bytes 2359304 | tf_op jit(solution)/shard_map/ppermute | solution.py:522
  8.5 36.6 %collective-permute-start = (bf16[128,768]{1,0:T(8,128)(2,1)}, bf16[128,768]{1,0:T(8,128)(2,1)}, u32[]{:S(2)}, u32[]{:S(2)}) collective-permute-start(bf16[128,768]{1,0:T(8,128)(2,1)} %slice.193), channel_id=1, source_target_pairs={{0,1},{1,2},{2,3},{4,5},{5,6},{6,7},{8,9},{9,10},{10,11},{12,13},{... | collective-permute-start | bytes 589832 | tf_op jit(solution)/shard_map/ppermute | solution.py:586
  25.1 19.7 %collective-permute-start.2 = (bf16[512,768]{1,0:T(8,128)(2,1)S(1)}, bf16[512,768]{1,0:T(8,128)(2,1)S(1)}, u32[]{:S(2)}, u32[]{:S(2)}) collective-permute-start(bf16[512,768]{1,0:T(8,128)(2,1)S(1)} %broadcast_select_fusion), channel_id=1, source_target_pairs={{0,1},{2,3},{4,5},{6,7},{8,9},{10,11},{12,13},{14,15},{16,17},{18,... | collective-permute-start | bytes 2359304 | tf_op jit(solution)/shard_map/ppermute | solution.py:524
  132.6 30.2 %collective-permute-start.5 = (bf16[128,768]{1,0:T(8,128)(2,1)S(1)}, bf16[128,768]{1,0:T(8,128)(2,1)}, u32[]{:S(2)}, u32[]{:S(2)}) collective-permute-start(bf16[128,768]{1,0:T(8,128)(2,1)S(1)} %slice.366), channel_id=1, source_target_pairs={{1,0},{2,1},{3,2},{5,4},{6,5},{7,6},{9,8},{10,9},{11,10},{13,12},{... | collective-permute-start | bytes 589832 | tf_op jit(solution)/shard_map/ppermute | solution.py:653
  133.9 24.1 %collective-permute-start.3 = (bf16[512,768]{1,0:T(8,128)(2,1)}, bf16[512,768]{1,0:T(8,128)(2,1)}, u32[]{:S(2)}, u32[]{:S(2)}) collective-permute-start(bf16[512,768]{1,0:T(8,128)(2,1)} %slice.365), channel_id=1, source_target_pairs={{1,0},{3,2},{5,4},{7,6},{9,8},{11,10},{13,12},{15,14},{17,16},{19,... | collective-permute-start | bytes 2359304 | tf_op jit(solution)/shard_map/ppermute | solution.py:534
  141.1 81.3 %collective-permute-start.26 = (bf16[16,96,768]{2,1,0:T(8,128)(2,1)}, bf16[16,96,768]{2,1,0:T(8,128)(2,1)}, u32[]{:S(2)}, u32[]{:S(2)}) collective-permute-start(bf16[16,96,768]{2,1,0:T(8,128)(2,1)} %bitcast.54), channel_id=1, source_target_pairs={{0,4},{4,0},{8,12},{12,8},{16,20},{20,16},{24,28},{28,24},{1,5},{5... | collective-permute-start | bytes 7077896 | tf_op jit(solution)/shard_map/ppermute | solution.py:490
  159.3 20.8 %collective-permute-start.4 = (bf16[512,768]{1,0:T(8,128)(2,1)S(1)}, bf16[512,768]{1,0:T(8,128)(2,1)S(1)}, u32[]{:S(2)}, u32[]{:S(2)}) collective-permute-start(bf16[512,768]{1,0:T(8,128)(2,1)S(1)} %fusion.41), channel_id=1, source_target_pairs={{2,0},{6,4},{10,8},{14,12},{18,16},{22,20},{26,24},{30,28}} | collective-permute-start | bytes 2359304 | tf_op jit(solution)/shard_map/ppermute | solution.py:535
  192.2 34.8 %collective-permute-start.6 = (bf16[16,104,768]{2,1,0:T(8,128)(2,1)}, bf16[16,104,768]{2,1,0:T(8,128)(2,1)}, u32[]{:S(2)}, u32[]{:S(2)}) collective-permute-start(bf16[16,104,768]{2,1,0:T(8,128)(2,1)} %bitcast.53), channel_id=1, source_target_pairs={{0,4},{4,0},{8,12},{12,8},{16,20},{20,16},{24,28},{28,24},{1,5},{5... | collective-permute-start | bytes 7667720 | tf_op jit(solution)/shard_map/ppermute | solution.py:490
  197.8 32.1 %collective-permute-start.16 = (bf16[16,96,768]{2,1,0:T(8,128)(2,1)}, bf16[16,96,768]{2,1,0:T(8,128)(2,1)}, u32[]{:S(2)}, u32[]{:S(2)}) collective-permute-start(bf16[16,96,768]{2,1,0:T(8,128)(2,1)} %bitcast.55), channel_id=1, source_target_pairs={{0,4},{4,0},{8,12},{12,8},{16,20},{20,16},{24,28},{28,24},{1,5},{5... | collective-permute-start | bytes 7077896 | tf_op jit(solution)/shard_map/ppermute | solution.py:490
  225.1 16.3 %collective-permute-start.27 = (bf16[8,96,768]{2,1,0:T(8,128)(2,1)S(1)}, bf16[8,96,768]{2,1,0:T(8,128)(2,1)S(1)}, u32[]{:S(2)}, u32[]{:S(2)}) collective-permute-start(bf16[8,96,768]{2,1,0:T(8,128)(2,1)S(1)} %get-tuple-element.78), channel_id=1, source_target_pairs={{0,8},{4,20},{8,0},{12,28},{16,24},{20,4},{24,16},{28,12},{1,9},{5... | collective-permute-start | bytes 3538952 | tf_op jit(solution)/shard_map/ppermute | solution.py:490
  229.5 31.9 %collective-permute-start.7 = (bf16[8,104,768]{2,1,0:T(8,128)(2,1)S(1)}, bf16[8,104,768]{2,1,0:T(8,128)(2,1)S(1)}, u32[]{:S(2)}, u32[]{:S(2)}) collective-permute-start(bf16[8,104,768]{2,1,0:T(8,128)(2,1)S(1)} %get-tuple-element.69), channel_id=1, source_target_pairs={{0,8},{4,20},{8,0},{12,28},{16,24},{20,4},{24,16},{28,12},{1,9},{5... | collective-permute-start | bytes 3833864 | tf_op jit(solution)/shard_map/ppermute | solution.py:490
  232.2 48.6 %collective-permute-start.17 = (bf16[8,96,768]{2,1,0:T(8,128)(2,1)S(1)}, bf16[8,96,768]{2,1,0:T(8,128)(2,1)S(1)}, u32[]{:S(2)}, u32[]{:S(2)}) collective-permute-start(bf16[8,96,768]{2,1,0:T(8,128)(2,1)S(1)} %get-tuple-element.84), channel_id=1, source_target_pairs={{0,8},{4,20},{8,0},{12,28},{16,24},{20,4},{24,16},{28,12},{1,9},{5... | collective-permute-start | bytes 3538952 | tf_op jit(solution)/shard_map/ppermute | solution.py:490
  241.7 41.4 %collective-permute-start.28 = (bf16[4,96,768]{2,1,0:T(8,128)(2,1)S(1)}, bf16[4,96,768]{2,1,0:T(8,128)(2,1)S(1)}, u32[]{:S(2)}, u32[]{:S(2)}) collective-permute-start(bf16[4,96,768]{2,1,0:T(8,128)(2,1)S(1)} %get-tuple-element.76), channel_id=1, source_target_pairs={{0,16},{4,12},{8,24},{12,4},{16,0},{20,28},{24,8},{28,20},{1,17},{... | collective-permute-start | bytes 1769480 | tf_op jit(solution)/shard_map/ppermute | solution.py:490
  261.7 21.6 %collective-permute-start.8 = (bf16[4,104,768]{2,1,0:T(8,128)(2,1)S(1)}, bf16[4,104,768]{2,1,0:T(8,128)(2,1)S(1)}, u32[]{:S(2)}, u32[]{:S(2)}) collective-permute-start(bf16[4,104,768]{2,1,0:T(8,128)(2,1)S(1)} %get-tuple-element.67), channel_id=1, source_target_pairs={{0,16},{4,12},{8,24},{12,4},{16,0},{20,28},{24,8},{28,20},{1,17},{... | collective-permute-start | bytes 1916936 | tf_op jit(solution)/shard_map/ppermute | solution.py:490
  283.4 21.4 %collective-permute-start.9 = (bf16[2,104,768]{2,1,0:T(8,128)(2,1)S(1)}, bf16[2,104,768]{2,1,0:T(8,128)(2,1)S(1)}, u32[]{:S(2)}, u32[]{:S(2)}) collective-permute-start(bf16[2,104,768]{2,1,0:T(8,128)(2,1)S(1)} %get-tuple-element.88), channel_id=1, source_target_pairs={{0,1},{1,0},{2,3},{3,2},{4,5},{5,4},{6,7},{7,6},{8,9},{9,8},{10,11... | collective-permute-start | bytes 958472 | tf_op jit(solution)/shard_map/ppermute | solution.py:490
  291.3 17.9 %collective-permute-start.19 = (bf16[2,96,768]{2,1,0:T(8,128)(2,1)S(1)}, bf16[2,96,768]{2,1,0:T(8,128)(2,1)S(1)}, u32[]{:S(2)}, u32[]{:S(2)}) collective-permute-start(bf16[2,96,768]{2,1,0:T(8,128)(2,1)S(1)} %get-tuple-element.92), channel_id=1, source_target_pairs={{0,1},{1,0},{2,3},{3,2},{4,5},{5,4},{6,7},{7,6},{8,9},{9,8},{10,11... | collective-permute-start | bytes 884744 | tf_op jit(solution)/shard_map/ppermute | solution.py:490
  293.2 36.8 %collective-permute-start.30 = (bf16[1,96,768]{2,1,0:T(8,128)(2,1)S(1)}, bf16[1,96,768]{2,1,0:T(8,128)(2,1)S(1)}, u32[]{:S(2)}, u32[]{:S(2)}) collective-permute-start(bf16[1,96,768]{2,1,0:T(8,128)(2,1)S(1)} %add_convert_fusion.19), channel_id=1, source_target_pairs={{0,2},{1,3},{2,0},{3,1},{4,6},{5,7},{6,4},{7,5},{8,10},{9,11},{10,... | collective-permute-start | bytes 442376 | tf_op jit(solution)/shard_map/ppermute | solution.py:490
  304.9 13.2 %collective-permute-start.10 = (bf16[1,104,768]{2,1,0:T(8,128)(2,1)S(1)}, bf16[1,104,768]{2,1,0:T(8,128)(2,1)S(1)}, u32[]{:S(2)}, u32[]{:S(2)}) collective-permute-start(bf16[1,104,768]{2,1,0:T(8,128)(2,1)S(1)} %add_convert_fusion.16), channel_id=1, source_target_pairs={{0,2},{1,3},{2,0},{3,1},{4,6},{5,7},{6,4},{7,5},{8,10},{9,11},{10,... | collective-permute-start | bytes 479240 | tf_op jit(solution)/shard_map/ppermute | solution.py:490
  309.2 12.1 %collective-permute-start.20 = (bf16[1,96,768]{2,1,0:T(8,128)(2,1)S(1)}, bf16[1,96,768]{2,1,0:T(8,128)(2,1)S(1)}, u32[]{:S(2)}, u32[]{:S(2)}) collective-permute-start(bf16[1,96,768]{2,1,0:T(8,128)(2,1)S(1)} %add_convert_fusion.22), channel_id=1, source_target_pairs={{0,2},{1,3},{2,0},{3,1},{4,6},{5,7},{6,4},{7,5},{8,10},{9,11},{10,... | collective-permute-start | bytes 442376 | tf_op jit(solution)/shard_map/ppermute | solution.py:490
  321.3 12.7 %collective-permute-start.21 = (bf16[1,96,768]{2,1,0:T(8,128)(2,1)S(1)}, bf16[1,96,768]{2,1,0:T(8,128)(2,1)S(1)}, u32[]{:S(2)}, u32[]{:S(2)}) collective-permute-start(bf16[1,96,768]{2,1,0:T(8,128)(2,1)S(1)} %get-tuple-element.56), channel_id=1, source_target_pairs={{0,2},{1,3},{2,0},{3,1},{4,6},{5,7},{6,4},{7,5},{8,10},{9,11},{10,... | collective-permute-start | bytes 442376 | tf_op jit(solution)/shard_map/ppermute | solution.py:490
  328.4 13.3 %collective-permute-start.12 = (bf16[2,104,768]{2,1,0:T(8,128)(2,1)S(1)}, bf16[2,104,768]{2,1,0:T(8,128)(2,1)S(1)}, u32[]{:S(2)}, u32[]{:S(2)}) collective-permute-start(bf16[2,104,768]{2,1,0:T(8,128)(2,1)S(1)} %pad_maximum_fusion.7), channel_id=1, source_target_pairs={{0,1},{1,0},{2,3},{3,2},{4,5},{5,4},{6,7},{7,6},{8,9},{9,8},{10,11... | collective-permute-start | bytes 958472 | tf_op jit(solution)/shard_map/ppermute | solution.py:490
  330.7 11.6 %collective-permute-start.31 = (bf16[1,96,768]{2,1,0:T(8,128)(2,1)S(1)}, bf16[1,96,768]{2,1,0:T(8,128)(2,1)S(1)}, u32[]{:S(2)}, u32[]{:S(2)}) collective-permute-start(bf16[1,96,768]{2,1,0:T(8,128)(2,1)S(1)} %get-tuple-element.54), channel_id=1, source_target_pairs={{0,2},{1,3},{2,0},{3,1},{4,6},{5,7},{6,4},{7,5},{8,10},{9,11},{10,... | collective-permute-start | bytes 442376 | tf_op jit(solution)/shard_map/ppermute | solution.py:490
  334.0 14.1 %collective-permute-start.22 = (bf16[2,96,768]{2,1,0:T(8,128)(2,1)S(1)}, bf16[2,96,768]{2,1,0:T(8,128)(2,1)S(1)}, u32[]{:S(2)}, u32[]{:S(2)}) collective-permute-start(bf16[2,96,768]{2,1,0:T(8,128)(2,1)S(1)} %pad_maximum_fusion.8), channel_id=1, source_target_pairs={{0,1},{1,0},{2,3},{3,2},{4,5},{5,4},{6,7},{7,6},{8,9},{9,8},{10,11... | collective-permute-start | bytes 884744 | tf_op jit(solution)/shard_map/ppermute | solution.py:490
  341.8 11.2 %collective-permute-start.13 = (bf16[4,104,768]{2,1,0:T(8,128)(2,1)S(1)}, bf16[4,104,768]{2,1,0:T(8,128)(2,1)S(1)}, u32[]{:S(2)}, u32[]{:S(2)}) collective-permute-start(bf16[4,104,768]{2,1,0:T(8,128)(2,1)S(1)} %pad_maximum_fusion.4), channel_id=1, source_target_pairs={{0,16},{4,12},{8,24},{12,4},{16,0},{20,28},{24,8},{28,20},{1,17},{... | collective-permute-start | bytes 1916936 | tf_op jit(solution)/shard_map/ppermute | solution.py:490
  348.1 14.6 %collective-permute-start.23 = (bf16[4,96,768]{2,1,0:T(8,128)(2,1)S(1)}, bf16[4,96,768]{2,1,0:T(8,128)(2,1)S(1)}, u32[]{:S(2)}, u32[]{:S(2)}) collective-permute-start(bf16[4,96,768]{2,1,0:T(8,128)(2,1)S(1)} %pad_maximum_fusion.5), channel_id=1, source_target_pairs={{0,16},{4,12},{8,24},{12,4},{16,0},{20,28},{24,8},{28,20},{1,17},{... | collective-permute-start | bytes 1769480 | tf_op jit(solution)/shard_map/ppermute | solution.py:490
  352.6 22.8 %collective-permute-start.33 = (bf16[4,96,768]{2,1,0:T(8,128)(2,1)S(1)}, bf16[4,96,768]{2,1,0:T(8,128)(2,1)S(1)}, u32[]{:S(2)}, u32[]{:S(2)}) collective-permute-start(bf16[4,96,768]{2,1,0:T(8,128)(2,1)S(1)} %pad_maximum_fusion.6), channel_id=1, source_target_pairs={{0,16},{4,12},{8,24},{12,4},{16,0},{20,28},{24,8},{28,20},{1,17},{... | collective-permute-start | bytes 1769480 | tf_op jit(solution)/shard_map/ppermute | solution.py:490
  353.2 26.8 %collective-permute-start.14 = (bf16[8,104,768]{2,1,0:T(8,128)(2,1)S(1)}, bf16[8,104,768]{2,1,0:T(8,128)(2,1)S(1)}, u32[]{:S(2)}, u32[]{:S(2)}) collective-permute-start(bf16[8,104,768]{2,1,0:T(8,128)(2,1)S(1)} %pad_maximum_fusion), channel_id=1, source_target_pairs={{0,8},{4,20},{8,0},{12,28},{16,24},{20,4},{24,16},{28,12},{1,9},{5... | collective-permute-start | bytes 3833864 | tf_op jit(solution)/shard_map/ppermute | solution.py:490
  362.9 23.9 %collective-permute-start.24 = (bf16[8,96,768]{2,1,0:T(8,128)(2,1)S(1)}, bf16[8,96,768]{2,1,0:T(8,128)(2,1)S(1)}, u32[]{:S(2)}, u32[]{:S(2)}) collective-permute-start(bf16[8,96,768]{2,1,0:T(8,128)(2,1)S(1)} %pad_maximum_fusion.1), channel_id=1, source_target_pairs={{0,8},{4,20},{8,0},{12,28},{16,24},{20,4},{24,16},{28,12},{1,9},{5... | collective-permute-start | bytes 3538952 | tf_op jit(solution)/shard_map/ppermute | solution.py:490
  375.5 23.9 %collective-permute-start.34 = (bf16[8,96,768]{2,1,0:T(8,128)(2,1)S(1)}, bf16[8,96,768]{2,1,0:T(8,128)(2,1)S(1)}, u32[]{:S(2)}, u32[]{:S(2)}) collective-permute-start(bf16[8,96,768]{2,1,0:T(8,128)(2,1)S(1)} %pad_maximum_fusion.2), channel_id=1, source_target_pairs={{0,8},{4,20},{8,0},{12,28},{16,24},{20,4},{24,16},{28,12},{1,9},{5... | collective-permute-start | bytes 3538952 | tf_op jit(solution)/shard_map/ppermute | solution.py:490
  381.1 51.1 %collective-permute-start.15 = (bf16[16,104,768]{2,1,0:T(8,128)(2,1)}, bf16[16,104,768]{2,1,0:T(8,128)(2,1)}, u32[]{:S(2)}, u32[]{:S(2)}) collective-permute-start(bf16[16,104,768]{2,1,0:T(8,128)(2,1)} %constant_dynamic-update-slice_fusion.6), channel_id=1, source_target_pairs={{0,4},{4,0},{8,12},{12,8},{16,20},{20,16},{24,28},{28,24},{1,5},{5... | collective-permute-start | bytes 7667720 | tf_op jit(solution)/shard_map/ppermute | solution.py:490
  386.8 23.0 %collective-permute-start.25 = (bf16[16,96,768]{2,1,0:T(8,128)(2,1)S(1)}, bf16[16,96,768]{2,1,0:T(8,128)(2,1)S(1)}, u32[]{:S(2)}, u32[]{:S(2)}) collective-permute-start(bf16[16,96,768]{2,1,0:T(8,128)(2,1)S(1)} %constant_dynamic-update-slice_fusion.11), channel_id=1, source_target_pairs={{0,4},{4,0},{8,12},{12,8},{16,20},{20,16},{24,28},{28,24},{1,5},{5... | collective-permute-start | bytes 7077896 | tf_op jit(solution)/shard_map/ppermute | solution.py:490
  400.4 21.5 %collective-permute-start.35 = (bf16[16,96,768]{2,1,0:T(8,128)(2,1)}, bf16[16,96,768]{2,1,0:T(8,128)(2,1)}, u32[]{:S(2)}, u32[]{:S(2)}) collective-permute-start(bf16[16,96,768]{2,1,0:T(8,128)(2,1)} %constant_dynamic-update-slice_fusion.16), channel_id=1, source_target_pairs={{0,4},{4,0},{8,12},{12,8},{16,20},{20,16},{24,28},{28,24},{1,5},{5... | collective-permute-start | bytes 7077896 | tf_op jit(solution)/shard_map/ppermute | solution.py:490
  (56 other events, 557.2 us)

commit v2 on v1

--- a/solution.py
+++ b/solution.py
@@ -87,59 +87,80 @@
     return jnp.where((lane >= h * HD) & (lane < (h + 1) * HD), x, jnp.zeros_like(x))
 
 
+def both_heads(x):
+    return jnp.concatenate([head_part(x, 0), head_part(x, 1)], axis=0)
+
+
+def twice(x):
+    return jnp.concatenate([x, x], axis=1)
+
+
+def key_chunks(reach, tail, b):
+    first = [(True, slice(c, c + 128), slice(c, c + 128)) for c in range(0, reach, 128)]
+    band = [
+        (False, slice(BQ * b + c, BQ * b + c + 128), slice(c, c + 128))
+        for c in range(0, tail + BQ, 128)
+    ]
+    return first + band
+
+
 def attend_kernel(
     pos_ref, count_ref, prefix_ref, lens_ref,
     q_ref, k_ref, v_ref, kx_ref, vx_ref,
-    out_ref, lse_ref,
-    bias_a, bias_b, k_ext, v_ext_t, v0_t,
+    out_ref, turned_ref, lse_ref,
+    bias_a, bias_b, k_ext, v_ext_t, v0_t, scores,
     *, rows, reach, tail,
 ):
     @pl.when(pl.program_id(0) == 0)
     def _():
         fill_bias(pos_ref, count_ref, prefix_ref, lens_ref, bias_a, bias_b, rows, reach, tail)
 
-    blocks = rows // BQ
     k_ext[:tail] = kx_ref[:tail]
     k_ext[tail:] = k_ref[...]
     v_ext_t[:, :tail] = transposed(vx_ref[:tail])
     v_ext_t[:, tail:] = transposed(v_ref[...])
     v0_t[...] = transposed(vx_ref[tail:])
-    k0 = kx_ref[tail:]
-    for b in range(blocks):
-        query = q_ref[BQ * b : BQ * b + BQ, :] * jnp.asarray(HD**-0.5, bf16)
-        k_band = k_ext[BQ * b : BQ * b + BQ + tail, :]
-        outs = []
-        for h in range(2):
-            part = head_part(query, h)
-            s_a = dot(k0, part, NT) + bias_a[b]
-            s_b = dot(k_band, part, NT) + bias_b[b]
-            top = jnp.maximum(
-                jnp.max(s_a, axis=0, keepdims=True), jnp.max(s_b, axis=0, keepdims=True)
-            )
-            p_a = jnp.exp(s_a - top)
-            p_b = jnp.exp(s_b - top)
-            total = jnp.sum(p_a, axis=0, keepdims=True) + jnp.sum(p_b, axis=0, keepdims=True)
-            hs = slice(h * HD, h * HD + HD)
-            o = dot(v0_t[hs, :], p_a.astype(bf16), NN) + dot(
-                v_ext_t[hs, BQ * b : BQ * b + BQ + tail], p_b.astype(bf16), NN
-            )
-            outs.append(o * (1.0 / total))
-            lse_ref[0, b, h : h + 1, :] = top + jnp.log(total)
-        out_ref[BQ * b : BQ * b + BQ, :] = jnp.concatenate(outs, axis=0).T.astype(bf16)
+    for b in range(rows // BQ):
+        at = slice(BQ * b, BQ * b + BQ)
+        parts = both_heads(q_ref[at, :] * jnp.asarray(HD**-0.5, bf16))
+        chunks = key_chunks(reach, tail, b)
+        tops = None
+        for i, (first, keys, biased) in enumerate(chunks):
+            k = kx_ref[tail + keys.start : tail + keys.stop] if first else k_ext[keys, :]
+            bias = bias_a[b, biased] if first else bias_b[b, biased]
+            s = dot(k, parts, NT) + twice(bias)
+            scores[b % 2, 128 * i : 128 * i + 128, :] = s
+            s = jnp.max(s.reshape(16, 8, 2 * BQ), axis=0)
+            tops = s if tops is None else jnp.maximum(tops, s)
+        top = jnp.max(tops, axis=0, keepdims=True)
+        sums = None
+        o = None
+        for i, (first, keys, _) in enumerate(chunks):
+            p = jnp.exp(scores[b % 2, 128 * i : 128 * i + 128, :] - top)
+            q = jnp.sum(p.reshape(16, 8, 2 * BQ), axis=0)
+            sums = q if sums is None else sums + q
+            v = v0_t[:, keys] if first else v_ext_t[:, keys]
+            p = dot(v, p.astype(bf16), NN)
+            o = p if o is None else o + p
+        total = jnp.sum(sums, axis=0, keepdims=True)
+        o = o * (1.0 / total)
+        o = jnp.concatenate([o[:HD, :BQ], o[HD:, BQ:]], axis=0)
+        turned_ref[0, b] = o
+        lse_ref[0, b] = top + jnp.log(total)
+        out_ref[at, :] = o.T.astype(bf16)
 
 
 def attend_back_kernel(
     pos_ref, count_ref, prefix_ref, lens_ref,
-    q_ref, k_ref, v_ref, kx_ref, vx_ref, g_ref, lse_ref,
+    q_ref, k_ref, v_ref, kx_ref, vx_ref, g_ref, turned_ref, lse_ref,
     dq_ref, dk_ref, dv_ref, dkx_ref, dvx_ref,
-    bias_a, bias_b, k_ext, v_ext, k_ext_t, k0_t, dk_ext, dv_ext, dk0, dv0,
+    bias_a, bias_b, k_ext, v_ext, k_ext_t, k0_t, dk_ext, dv_ext, p_a, ds_a, p_b, ds_b, parts, gparts,
     *, rows, reach, tail,
 ):
     @pl.when(pl.program_id(0) == 0)
     def _():
         fill_bias(pos_ref, count_ref, prefix_ref, lens_ref, bias_a, bias_b, rows, reach, tail)
 
-    blocks = rows // BQ
     k_ext[:tail] = kx_ref[:tail]
     k_ext[tail:] = k_ref[...]
     v_ext[:tail] = vx_ref[:tail]
@@ -147,49 +168,48 @@
     k_ext_t[:, :tail] = transposed(kx_ref[:tail])
     k_ext_t[:, tail:] = transposed(k_ref[...])
     k0_t[...] = transposed(kx_ref[tail:])
-    k0 = kx_ref[tail:]
-    v0 = vx_ref[tail:]
     dk_ext[...] = jnp.zeros_like(dk_ext)
     dv_ext[...] = jnp.zeros_like(dv_ext)
     scale = HD**-0.5
-    for b in range(blocks):
+    for b in range(rows // BQ):
         at = slice(BQ * b, BQ * b + BQ)
+        both = slice(2 * BQ * b, 2 * BQ * b + 2 * BQ)
         band = slice(BQ * b, BQ * b + BQ + tail)
-        query = q_ref[at, :] * jnp.asarray(scale, bf16)
-        grad = g_ref[at, :]
-        k_band = k_ext[band, :]
-        v_band = v_ext[band, :]
-        outs = []
-        for h in range(2):
-            hs = slice(h * HD, h * HD + HD)
-            part = head_part(query, h)
-            gpart = head_part(grad, h)
-            lse = lse_ref[0, b, h : h + 1, :]
-            p_a = jnp.exp(dot(k0, part, NT) + bias_a[b] - lse)
-            p_b = jnp.exp(dot(k_band, part, NT) + bias_b[b] - lse)
-            dp_a = dot(v0, gpart, NT)
-            dp_b = dot(v_band, gpart, NT)
-            inner = jnp.sum(p_a * dp_a, axis=0, keepdims=True) + jnp.sum(
-                p_b * dp_b, axis=0, keepdims=True
-            )
-            ds_a = (p_a * (dp_a - inner)).astype(bf16)
-            ds_b = (p_b * (dp_b - inner)).astype(bf16)
-            dv_a = dot(p_a.astype(bf16), gpart, NN)
-            dk_a = dot(ds_a, part, NN)
-            if b == 0 and h == 0:
-                dv0[...] = dv_a
-                dk0[...] = dk_a
+        part = both_heads(q_ref[at, :] * jnp.asarray(scale, bf16))
+        gpart = both_heads(g_ref[at, :])
+        parts[both, :] = part
+        gparts[both, :] = gpart
+        inner = turned_ref[0, b] * g_ref[at, :].astype(f32).T
+        inner = jnp.concatenate(
+            [
+                jnp.sum(inner[:HD], axis=0, keepdims=True),
+                jnp.sum(inner[HD:], axis=0, keepdims=True),
+            ],
+            axis=1,
+        )
+        lse = lse_ref[0, b]
+        for first, keys, biased in key_chunks(reach, tail, b):
+            there = slice(tail + keys.start, tail + keys.stop)
+            k = kx_ref[there] if first else k_ext[keys, :]
+            v = vx_ref[there] if first else v_ext[keys, :]
+            bias = bias_a[b, biased] if first else bias_b[b, biased]
+            p = jnp.exp(dot(k, part, NT) + twice(bias) - lse)
+            ds = (p * (dot(v, gpart, NT) - inner)).astype(bf16)
+            if first:
+                p_a[keys, both] = p.astype(bf16)
+                ds_a[keys, both] = ds
             else:
-                dv0[...] += dv_a
-                dk0[...] += dk_a
-            dv_ext[band, :] += dot(p_b.astype(bf16), gpart, NN)
-            dk_ext[band, :] += dot(ds_b, part, NN)
-            outs.append(dot(k0_t[hs, :], ds_a, NN) + dot(k_ext_t[hs, band], ds_b, NN))
-        dq_ref[at, :] = (jnp.concatenate(outs, axis=0) * scale).T.astype(bf16)
+                p_b[biased, both] = p.astype(bf16)
+                ds_b[biased, both] = ds
+        dv_ext[band, :] += dot(p_b[:, both], gpart, NN)
+        dk_ext[band, :] += dot(ds_b[:, both], part, NN)
+        o = dot(k0_t[...], ds_a[:, both], NN) + dot(k_ext_t[:, band], ds_b[:, both], NN)
+        o = jnp.concatenate([o[:HD, :BQ], o[HD:, BQ:]], axis=0) * scale
+        dq_ref[at, :] = o.T.astype(bf16)
+    dkx_ref[tail:] = dot(ds_a[...], parts[...], NN).astype(bf16)
+    dvx_ref[tail:] = dot(p_a[...], gparts[...], NN).astype(bf16)
     dkx_ref[:tail] = dk_ext[:tail].astype(bf16)
-    dkx_ref[tail:] = dk0[...].astype(bf16)
     dvx_ref[:tail] = dv_ext[:tail].astype(bf16)
-    dvx_ref[tail:] = dv0[...].astype(bf16)
     dk_ref[...] = dk_ext[tail:].astype(bf16)
     dv_ref[...] = dv_ext[tail:].astype(bf16)
 
@@ -217,7 +237,8 @@
             ],
             out_specs=[
                 column_block(rows),
-                pl.BlockSpec((1, blocks, 2, BQ), lambda i, *_: (i, 0, 0, 0)),
+                pl.BlockSpec((1, blocks, 128, BQ), lambda i, *_: (i, 0, 0, 0)),
+                pl.BlockSpec((1, blocks, 1, 2 * BQ), lambda i, *_: (i, 0, 0, 0)),
             ],
             scratch_shapes=[
                 pltpu.VMEM((blocks, reach, BQ), f32),
@@ -225,17 +246,19 @@
                 pltpu.VMEM((tail + rows, 128), bf16),
                 pltpu.VMEM((128, tail + rows), bf16),
                 pltpu.VMEM((128, reach), bf16),
+                pltpu.VMEM((2, reach + tail + BQ, 2 * BQ), f32),
             ],
         ),
         out_shape=[
             jax.ShapeDtypeStruct((rows, width), bf16),
-            jax.ShapeDtypeStruct((steps, blocks, 2, BQ), f32),
+            jax.ShapeDtypeStruct((steps, blocks, 128, BQ), f32),
+            jax.ShapeDtypeStruct((steps, blocks, 1, 2 * BQ), f32),
         ],
         name="attend",
     )(*scalars, qkv, qkv, qkv, kvx, kvx)
 
 
-def attend_back(scalars, qkv, kvx, grad, lse, rows, reach, tail):
+def attend_back(scalars, qkv, kvx, grad, turned, lse, rows, reach, tail):
     width = qkv.shape[1] // 3
     steps = width // 128
     blocks = rows // BQ
@@ -252,7 +275,8 @@
                 column_block(extra),
                 column_block(extra, steps),
                 column_block(rows),
-                pl.BlockSpec((1, blocks, 2, BQ), lambda i, *_: (i, 0, 0, 0)),
+                pl.BlockSpec((1, blocks, 128, BQ), lambda i, *_: (i, 0, 0, 0)),
+                pl.BlockSpec((1, blocks, 1, 2 * BQ), lambda i, *_: (i, 0, 0, 0)),
             ],
             out_specs=[
                 column_block(rows),
@@ -270,8 +294,12 @@
                 pltpu.VMEM((128, reach), bf16),
                 pltpu.VMEM((tail + rows, 128), f32),
                 pltpu.VMEM((tail + rows, 128), f32),
-                pltpu.VMEM((reach, 128), f32),
-                pltpu.VMEM((reach, 128), f32),
+                pltpu.VMEM((reach, 2 * rows), bf16),
+                pltpu.VMEM((reach, 2 * rows), bf16),
+                pltpu.VMEM((tail + BQ, 2 * rows), bf16),
+                pltpu.VMEM((tail + BQ, 2 * rows), bf16),
+                pltpu.VMEM((2 * rows, 128), bf16),
+                pltpu.VMEM((2 * rows, 128), bf16),
             ],
         ),
         out_shape=[
@@ -282,7 +310,7 @@
             jax.ShapeDtypeStruct((extra, width), bf16),
         ],
         name="attend_back",
-    )(*scalars, qkv, qkv, qkv, kvx, kvx, grad, lse)
+    )(*scalars, qkv, qkv, qkv, kvx, kvx, grad, turned, lse)
 
 
 def mask_of(side, me):
@@ -386,25 +414,31 @@
     )(me, dqkv, normed, dkvx, normed_x, attended, grad_branch, small)
 
 
-def slab_of(me_ref, f_ref, g_ref, o):
-    far = (o >> 2) != me_ref[0]
-    low = me_ref[3]
-    pieces = []
-    for c in range(PIECES):
-        f = f_ref[0, c ^ low, :ROWS, :].astype(f32)
-        g = g_ref[0, c ^ low, :ROWS, :].astype(f32)
-        pieces.append(jnp.where(far, g, f))
+def slab_of(me_ref, ref):
+    pieces = [ref[0, c ^ me_ref[3], :ROWS, :].astype(f32) for c in range(PIECES)]
     return jnp.concatenate(pieces, axis=0)
 
 
 def spread_kernel(me_ref, f_ref, g_ref, out_ref, *, turned):
-    slab = slab_of(me_ref, f_ref, g_ref, pl.program_id(0))
-    out_ref[...] = slab.T if turned else slab
+    o = pl.program_id(0)
+    for ref, mine in ((f_ref, (o >> 2) == me_ref[0]), (g_ref, (o >> 2) != me_ref[0])):
+
+        @pl.when(mine)
+        def _():
+            slab = slab_of(me_ref, ref)
+            out_ref[...] = slab.T if turned else slab
 
 
 def half_specs(rows, width):
-    spec = pl.BlockSpec((1, PIECES, rows, width), lambda o, me: (place_of(o, me) & 3, 0, 0, 0))
-    return [spec, spec]
+    def block(o, me, other):
+        side = me[0] ^ other
+        rest = jnp.where(side == 0, jnp.minimum(o, 3), jnp.maximum(o, 4))
+        return (place_of(rest, me) & 3, 0, 0, 0)
+
+    return [
+        pl.BlockSpec((1, PIECES, rows, width), lambda o, me: block(o, me, 0)),
+        pl.BlockSpec((1, PIECES, rows, width), lambda o, me: block(o, me, 1)),
+    ]
 
 
 def spread(me, near, far, turned):
@@ -428,24 +462,20 @@
 
 def mixed_spread_kernel(me_ref, f_ref, g_ref, qkv_ref, out_ref, small_ref):
     o = pl.program_id(0)
-    slab = slab_of(me_ref, f_ref, g_ref, o)
-
-    @pl.when(o < 6)
-    def _():
-        qkv_ref[...] = slab.T
-
-    @pl.when(o >= 6)
-    def _():
-        out_ref[...] = slab
-
-    @pl.when(o == 0)
-    def _():
-        far = me_ref[0] != 0
-        for c in range(2):
-            at = c ^ (me_ref[3])
-            f = f_ref[0, at, ROWS:, :].astype(f32)
-            g = g_ref[0, at, ROWS:, :].astype(f32)
-            small_ref[EXTRA * c : EXTRA * c + EXTRA, :] = jnp.where(far, g, f)
+    for ref, mine in ((f_ref, (o >> 2) == me_ref[0]), (g_ref, (o >> 2) != me_ref[0])):
+
+        @pl.when(mine & (o < 6))
+        def _():
+            qkv_ref[...] = slab_of(me_ref, ref).T
+
+        @pl.when(mine & (o >= 6))
+        def _():
+            out_ref[...] = slab_of(me_ref, ref)
+
+        @pl.when(mine & (o == 0))
+        def _():
+            for c in range(2):
+                small_ref[EXTRA * c : EXTRA * c + EXTRA, :] = ref[0, c ^ me_ref[3], ROWS:, :].astype(f32)
 
 
 def mixed_spread(me, near, far):
@@ -494,37 +524,58 @@
     return (a.astype(f32) + b.astype(f32)).astype(bf16)
 
 
-def total_halves(near, far, cube):
-    if not cube:
-        return lax.psum((near, far), ("grp", "pos"))
-    shape = near.shape
-    count = shape[0] * shape[1]
-    keep = near.reshape((count,) + shape[2:])
-    send = far.reshape((count,) + shape[2:])
-    for step in range(5):
-        got = hop(send, step)
-        half = count // 2
-        if step < 4:
-            send = added(keep[half:], got[half:])
-            keep = added(keep[:half], got[:half])
-            count = half
+def tied(*values):
+    return lax.optimization_barrier(values)
+
+
+class Sum:
+    def __init__(self, far, cube):
+        self.shape = far.shape
+        self.cube = cube
+        self.stage = 0
+        self.keep = None
+        self.send = far.reshape((16,) + far.shape[2:])
+        self.launch()
+
+    def launch(self):
+        if self.cube and self.stage < 10:
+            self.got = hop(self.send, self.stage if self.stage < 5 else 9 - self.stage)
+
+    def give(self, near):
+        self.keep = near.reshape(self.send.shape)
+
+    def settle(self):
+        got = self.got
+        half = self.keep.shape[0] // 2
+        if self.stage < 4:
+            self.send = added(self.keep[half:], got[half:])
+            self.keep = added(self.keep[:half], got[:half])
+        elif self.stage == 4:
+            self.keep = self.send = added(self.keep, got)
+        elif self.stage < 9:
+            self.keep = self.send = jnp.concatenate([self.keep, got], axis=0)
         else:
-            keep = added(keep, got)
-    for step in (4, 3, 2, 1):
-        keep = jnp.concatenate([keep, hop(keep, step)], axis=0)
-    other = hop(keep, 0)
-    return keep.reshape(shape), other.reshape(shape)
-
-
-def fetch_first(value, blocks, cube):
-    if cube and blocks == 1:
-        place = lax.axis_index("pos")
-        got = lax.ppermute(value, "pos", [(0, 2)])
-        here = jnp.where(place == 2, got, value)
-        got = lax.ppermute(here, "pos", [(0, 1), (2, 3)])
-        return jnp.where(place % 2 == 1, got, here)
-    rows = value.shape[0]
-    return lax.all_gather(value, "pos", axis=0, tiled=True)[: blocks * rows]
+            self.send = got
+        self.stage += 1
+
+    def halves(self):
+        if not self.cube:
+            near, far = lax.psum((self.keep, self.send), ("grp", "pos"))
+            return near.reshape(self.shape), far.reshape(self.shape)
+        while self.stage < 10:
+            advance((), self)
+        return self.keep.reshape(self.shape), self.send.reshape(self.shape)
+
+
+def advance(values, *sums):
+    sums = [one for one in sums if one.cube and one.stage < 10]
+    for one in sums:
+        one.settle()
+    states = [(one.keep, one.send) for one in sums]
+    values, states = tied(values, states)
+    for one, (one.keep, one.send) in zip(sums, states):
+        one.launch()
+    return values
 
 
 def return_first(partial, blocks, rows, cube):
@@ -586,20 +637,31 @@
     tail_in = lax.ppermute(
         hidden_in[rows - tail :], "pos", [(p, p + 1) for p in range(n_pos - 1)]
     )
-    first_in = fetch_first(hidden_in, blocks, cube)
+    two_step = cube and blocks == 1
+    if two_step:
+        got = lax.ppermute(hidden_in, "pos", [(0, 2)])
+    else:
+        got = lax.all_gather(hidden_in, "pos", axis=0, tiled=True)[: blocks * rows]
 
     inputs = hidden_in.astype(f32)
     xhat1, inv1 = norm_stats(inputs)
     normed1 = (xhat1 * gain1 + shift1).astype(bf16)
     bias = jnp.concatenate([b_query.astype(f32), jnp.zeros((width,), f32), b_value.astype(f32)])
     qkv = (dot(normed1, w_qkv, NN) + bias).astype(bf16)
+    qkv, got, cotangent = tied(qkv, got, cotangent)
+    if two_step:
+        here = jnp.where(place == 2, got, hidden_in)
+        got = lax.ppermute(here, "pos", [(0, 1), (2, 3)])
+    grad_activ = dot(cotangent, w_down, NT)
+    grad_activ, got, tail_in = tied(grad_activ, got, tail_in)
+    first_in = jnp.where(place % 2 == 1, got, here) if two_step else got
 
     inputs_x = jnp.concatenate([tail_in, first_in], axis=0).astype(f32)
     xhat1_x, _ = norm_stats(inputs_x)
     normed1_x = (xhat1_x * gain1 + shift1).astype(bf16)
     kvx = (dot(normed1_x, w_qkv[:, width:], NN) + bias[width:]).astype(bf16)
 
-    attended, lse = attend(scalars, qkv, kvx, rows, reach, tail)
+    attended, turned, lse = attend(scalars, qkv, kvx, rows, reach, tail)
 
     middle = inputs + dot(attended, w_out, NN) + b_out.astype(f32)
     xhat2, inv2 = norm_stats(middle)
@@ -609,27 +671,35 @@
     activ = activ.astype(bf16)
 
     down_far = outer_half(me, activ, cotangent, 1)
-    down_near = outer_half(me, activ, cotangent, 0)
-    down = total_halves(down_near, down_far, cube)
-
-    grad_activ = dot(cotangent, w_down, NT)
+    down_far, activ, cotangent, grad_activ = tied(down_far, activ, cotangent, grad_activ)
+    down = Sum(down_far, cube)
+    down.give(outer_half(me, activ, cotangent, 0))
+    grad_activ, activ = advance((grad_activ, activ), down)
+
     grad_pre = gelu_pull(grad_activ)[0].astype(bf16)
-
     up_far = outer_half(me, grad_pre, normed2, 1)
-    up_near = outer_half(me, grad_pre, normed2, 0)
-    up = total_halves(up_near, up_far, cube)
+    up_far, grad_pre, normed2 = tied(up_far, grad_pre, normed2)
+    up = Sum(up_far, cube)
+    grad_pre, normed2 = advance((grad_pre, normed2), down)
+    up.give(outer_half(me, grad_pre, normed2, 0))
+    (grad_pre,) = advance((grad_pre,), up)
 
     grad_normed2 = dot(grad_pre, w_up, NT)
     grad_middle = cotangent.astype(f32) + norm_back(grad_normed2, gain2, xhat2, inv2)
     grad_branch = grad_middle.astype(bf16)
     grad_attended = dot(grad_branch, w_out, NT).astype(bf16)
-    dq, dk, dv, dkx, dvx = attend_back(
-        scalars, qkv, kvx, grad_attended, lse, rows, reach, tail
-    )
+    (grad_attended,) = advance((grad_attended,), down)
+    grads = attend_back(scalars, qkv, kvx, grad_attended, turned, lse, rows, reach, tail)
+    dq, dk, dv, dkx, dvx = advance(grads, down, up)
     dqkv = jnp.concatenate([dq, dk, dv], axis=1)
     dkvx = jnp.concatenate([dkx, dvx], axis=1)
     grad_normed1 = dot(dqkv, w_qkv, NT)
     grad_normed1_x = dot(dkvx, w_qkv[:, width:], NT)
+    grad_normed1, grad_normed1_x = advance((grad_normed1, grad_normed1_x), down, up)
+
+    back_tail = lax.ppermute(
+        grad_normed1_x[:tail].astype(bf16), "pos", [(p + 1, p) for p in range(n_pos - 1)]
+    )
 
     small = jnp.concatenate(
         [
@@ -647,12 +717,13 @@
     ).reshape(2 * EXTRA, width)
     mixed_args = (me, dqkv, normed1, dkvx, normed1_x, attended, grad_branch, small)
     mixed_far = mixed_half(*mixed_args, 1)
-    mixed_near = mixed_half(*mixed_args, 0)
-    mixed = total_halves(mixed_near, mixed_far, cube)
-
-    back_tail = lax.ppermute(
-        grad_normed1_x[:tail].astype(bf16), "pos", [(p + 1, p) for p in range(n_pos - 1)]
-    )
+    (mixed_far,) = advance((mixed_far,), down, up)
+    mixed = Sum(mixed_far, cube)
+    mixed.give(mixed_half(*mixed_args, 0))
+    advance((), mixed, up)
+    advance((), mixed)
+    advance((), mixed, down, up)
+
     back_first = return_first(grad_normed1_x[tail:], blocks, rows, cube)
     grad_normed1 = (
         grad_normed1
@@ -663,9 +734,9 @@
 
     layer_out = (middle + dot(activ, w_down, NN) + b_down.astype(f32)).astype(bf16)
 
-    grad_w_down = spread(me, *down, False)
-    grad_w_up = spread(me, *up, True)
-    grad_w_qkv, grad_w_out, vectors = mixed_spread(me, *mixed)
+    grad_w_down = spread(me, *down.halves(), False)
+    grad_w_up = spread(me, *up.halves(), True)
+    grad_w_qkv, grad_w_out, vectors = mixed_spread(me, *mixed.halves())
     return (
         layer_out,
         input_grad,

time: 454 us -> 456 us (level)
  waiting for transfers between devices: 169 us -> 189 us
  local copies, waits for them, and re-layouts: 35.8 us -> 16 us
  Pallas kernels: 115 us -> 97.5 us
  other arithmetic: 36.8 us -> 53.4 us
    ppermute x30, waiting for transfers between devices: 129 us -> 166 us  [hop(): return lax.ppermute(value, axis, pairs)]
    ppermute x1, waiting for transfers between devices: 17.2 us -> 0.01 us  [return_first(): got = lax.ppermute(here.astype(bf16), 'pos', [(2, 0)])]
    unnamed x122 -> x129, local copies, waits for them, and re-layouts: 20.5 us -> 5.42 us
    ppermute x2, waiting for transfers between devices: 15.2 us -> 4.49 us  [the longest x1 4.49 us: body(): got = lax.ppermute(hidden_in, 'pos', [(0, 2)])]
    ppermute x1, waiting for transfers between devices: 7.22 us -> 16.1 us  [return_first(): lax.ppermute(low, 'pos', [(1, 0), (3, 2)]).astype(f32)]
    convert_element_type x0 -> x1, other arithmetic: none -> 8.68 us  [body(): grad_pre = gelu_pull(grad_activ)[0].astype(bf16)]
    convert_element_type x12 -> x15, other arithmetic: 8.5 us -> 16.1 us  [added(): return (a.astype(f32) + b.astype(f32)).astype(bf16)]
    pallas_call x1, Pallas kernels: 20.1 us -> 13.5 us  [attend(): pl.pallas_call(functools.partial(attend_kernel, rows=rows, reach=reach, t...]
  transfers between devices with their start and end apart: 36 -> 36, of which waited for: 21 -> 23; matrix products, arithmetic and copies ran while one was open for 14% -> 12% of each run, Pallas kernels for 13% -> 12%
where the time goes in v2:
time: 456 us; the launch traced here: 451 us
  waiting for transfers between devices  189 us (41%)
  Pallas kernels  97.5 us (21%)
  other arithmetic  53.4 us (12%)
  starting transfers between devices  50 us (11%)
  matrix products  41.5 us (9%)
  local copies, waits for them, and re-layouts  16 us (4%)
    ppermute x30, waiting for transfers between devices, hop(): return lax.ppermute(value, axis, pairs)  166 us
    dot_general x10, matrix products, dot(): return lax.dot_general(a, b, (dims, ((), ())), preferred_element_type=f32)  41.5 us
    ppermute x30, starting transfers between devices, hop(): return lax.ppermute(value, axis, pairs)  34.6 us
    pallas_call x4, Pallas kernels, outer_half(): pl.pallas_call(outer_kernel, grid_spec=pltpu.PrefetchScalarGridSpec(num_s...  22.6 us
    pallas_call x1, Pallas kernels, attend_back(): pl.pallas_call(functools.partial(attend_back_kernel, rows=rows, reach=rea...  19.2 us
    pallas_call x2, Pallas kernels, spread(): pl.pallas_call(functools.partial(spread_kernel, turned=turned), grid_spec...  17.8 us
    ppermute x1, waiting for transfers between devices, return_first(): lax.ppermute(low, 'pos', [(1, 0), (3, 2)]).astype(f32)  16.1 us
    convert_element_type x15, other arithmetic, added(): return (a.astype(f32) + b.astype(f32)).astype(bf16)  16.1 us
  transfers between devices with their start and end apart: 36, of which 23 were waited for; matrix products, arithmetic and copies ran while one was open for 12% of the time, Pallas kernels for 12%

profile of v2, /device:TPU:0, one launch (start us, length us, event | category | flops | bytes accessed | tf_op | source)
XLA Modules:
  0.0 450.9 jit_solution(13471440548633279606)
XLA Ops:
  0.7 7.0 %collective-permute-start = (bf16[512,768]{1,0:T(8,128)(2,1)}, bf16[512,768]{1,0:T(8,128)(2,1)}, u32[]{:S(2)}, u32[]{:S(2)}) collective-permute-start(bf16[512,768]{1,0:T(8,128)(2,1)} %param.18), channel_id=1, source_target_pairs={{0,2},{4,6},{8,10},{12,14},{16,18},{20,22},{24,26},{28,30}} | collective-permute-start | bytes 2359304 | tf_op jit(solution)/shard_map/ppermute | solution.py:642
  13.7 5.7 %fusion.7.q_ref.k_ref.v_ref = bf16[512,2304]{1,0:T(8,128)(2,1)} fusion(bf16[512,768]{1,0:T(8,128)(2,1)S(1)} %fusion.32.n_ref, bf16[768,2304]{1,0:T(8,128)(2,1)} %param.21, f32[2304]{0:T(1024)S(1)} %pad_maximum_fusion.13), kind=kOutput, calls=%fused_computation.12 | convolution fusion | flops 1814298624 | bytes 6693888 | tf_op jit(solution)/shard_map/dot_general | solution.py:24
  36.0 6.8 %fusion.49 = f32[512,3072]{1,0:T(8,128)} fusion(bf16[512,768]{1,0:T(8,128)(2,1)S(1)} %copy-done.18, bf16[3072,768]{1,0:T(8,128)(2,1)} %param.30), kind=kOutput, calls=%fused_computation.155 | convolution fusion | flops 2415919104 | bytes 11796480 | tf_op jit(solution)/shard_map/dot_general | solution.py:24
  53.2 13.5 %attend.1 = (bf16[512,768]{1,0:T(8,128)(2,1)}, f32[6,4,128,128]{3,2,1,0:T(8,128)}, f32[6,4,1,256]{3,2,1,0:T(1,128)}) custom-call(s32[1]{0:T(128)} %bitcast.pos_ref, s32[1]{0:T(128)S(6)} %copy.46.count_ref, s32[1]{0:T(128)S(6)} %copy.47.prefix_ref, s32[1,16]{1,0:T(1,128)} %lens_ref.3, bf16[512,2304]{1,0:T(8,128)(2,1)} %fusion.7.q_ref.k_ref.v_ref, ...), custom_call_target="tpu_custom_call" | custom-call | tf_op jit(solution)/shard_map/attend/pallas_call | solution.py:226
  70.4 8.9 %multiply_convert_fusion = (bf16[512,3072]{1,0:T(8,128)(2,1)}, f32[512,3072]{1,0:T(8,128)}) fusion(f32[3072]{0:T(1024)S(1)} %copy-done.32, bf16[512,768]{1,0:T(8,128)(2,1)S(1)} %add_convert_fusion.2.b_ref, bf16[768,3072]{1,0:T(8,128)(2,1)} %param.28), kind=kOutput, calls=%fused_computation.10 | convolution fusion | flops 2431647744 | bytes 14954496 | tf_op jit(solution)/shard_map/dot_general | solution.py:24
  79.4 5.7 %outer.4 = bf16[4,4,96,768]{3,2,1,0:T(8,128)(2,1)} custom-call(s32[4]{0:T(128)} %pad_add_fusion.me_ref, bf16[512,3072]{1,0:T(8,128)(2,1)} %get-tuple-element.124.a_ref, bf16[512,768]{1,0:T(8,128)(2,1)} %b_ref.1), custom_call_target="tpu_custom_call" | custom-call | tf_op jit(solution)/shard_map/outer/pallas_call | solution.py:342
  85.0 5.6 %outer.5 = bf16[4,4,96,768]{3,2,1,0:T(8,128)(2,1)} custom-call(s32[4]{0:T(128)} %pad_add_fusion.me_ref, bf16[512,3072]{1,0:T(8,128)(2,1)} %get-tuple-element.124.a_ref, bf16[512,768]{1,0:T(8,128)(2,1)} %b_ref.1), custom_call_target="tpu_custom_call" | custom-call | tf_op jit(solution)/shard_map/outer/pallas_call | solution.py:342
  96.2 8.7 %fusion.6.a_ref = bf16[512,3072]{1,0:T(8,128)(2,1)} fusion(f32[512,3072]{1,0:T(8,128)} %fusion.49, f32[512,3072]{1,0:T(8,128)} %get-tuple-element.270, f32[3072]{0:T(1024)S(1)} %copy-done.33), kind=kLoop, calls=%fused_computation.8 | loop fusion | flops 33030144 | bytes 15740928 | tf_op jit(solution)/shard_map/convert_element_type | solution.py:679
  104.9 5.6 %outer.6 = bf16[4,4,96,768]{3,2,1,0:T(8,128)(2,1)} custom-call(s32[4]{0:T(128)} %pad_add_fusion.me_ref, bf16[512,3072]{1,0:T(8,128)(2,1)} %fusion.6.a_ref, bf16[512,768]{1,0:T(8,128)(2,1)} %copy-done.17), custom_call_target="tpu_custom_call" | custom-call | tf_op jit(solution)/shard_map/outer/pallas_call | solution.py:342
  112.5 14.9 %collective-permute-done.4 = bf16[8,96,768]{2,1,0:T(8,128)(2,1)S(1)} collective-permute-done((bf16[8,96,768]{2,1,0:T(8,128)(2,1)}, bf16[8,96,768]{2,1,0:T(8,128)(2,1)S(1)}, u32[]{:S(2)}, u32[]{:S(2)}) %collective-permute-start.4) | collective-permute-done | bytes 1179680 | tf_op jit(solution)/shard_map/ppermute | solution.py:520
  131.3 5.6 %outer.7 = bf16[4,4,96,768]{3,2,1,0:T(8,128)(2,1)} custom-call(s32[4]{0:T(128)} %pad_add_fusion.me_ref, bf16[512,3072]{1,0:T(8,128)(2,1)} %fusion.6.a_ref, bf16[512,768]{1,0:T(8,128)(2,1)} %copy-done.17), custom_call_target="tpu_custom_call" | custom-call | tf_op jit(solution)/shard_map/outer/pallas_call | solution.py:342
  146.0 6.0 %multiply_reduce_fusion = (f32[768]{0:T(1024)}, f32[512]{0:T(512)S(1)}, f32[512]{0:T(512)S(1)}, f32[768]{0:T(1024)}, f32[512,768]{1,0:T(8,128)S(1)}) fusion(f32[512,768]{1,0:T(8,128)S(1)} %get-tuple-element.268, f32[512]{0:T(512)S(1)} %copy-done.45, f32[512]{0:T(512)S(1)} %copy-done.43, f32[768]{0:T(1024)S(1)} %copy-done.38, ...), kind=kOutput, calls=%fused_computation.67 | convolution fusion | flops 2419455488 | bytes 11027456 | tf_op jit(solution)/shard_map/dot_general | solution.py:24
  161.3 19.2 %attend_back.1 = (bf16[512,768]{1,0:T(8,128)(2,1)}, bf16[512,768]{1,0:T(8,128)(2,1)}, bf16[512,768]{1,0:T(8,128)(2,1)}, bf16[640,768]{1,0:T(8,128)(2,1)}, bf16[640,768]{1,0:T(8,128)(2,1)}) custom-call(s32[1]{0:T(128)} %bitcast.pos_ref, s32[1]{0:T(128)S(6)} %copy.46.count_ref, s32[1]{0:T(128)S(6)} %copy.47.prefix_ref, s32[1,16]{1,0:T(1,128)} %lens_ref.3, ...), custom_call_target="tpu_custom_call" | custom-call | tf_op jit(solution)/shard_map/attend_back/pallas_call | solution.py:266
  204.6 16.1 %collective-permute-done.11 = bf16[512,768]{1,0:T(8,128)(2,1)S(1)} collective-permute-done((bf16[512,768]{1,0:T(8,128)(2,1)S(1)}, bf16[512,768]{1,0:T(8,128)(2,1)S(1)}, u32[]{:S(2)}, u32[]{:S(2)}) %collective-permute-start.11) | collective-permute-done | bytes 786464 | tf_op jit(solution)/shard_map/ppermute | solution.py:585
  231.4 18.3 %collective-permute-done.14 = bf16[1,96,768]{2,1,0:T(8,128)(2,1)S(1)} collective-permute-done((bf16[1,96,768]{2,1,0:T(8,128)(2,1)S(1)}, bf16[1,96,768]{2,1,0:T(8,128)(2,1)S(1)}, u32[]{:S(2)}, u32[]{:S(2)}) %collective-permute-start.14) | collective-permute-done | bytes 147488 | tf_op jit(solution)/shard_map/ppermute | solution.py:520
  256.7 7.7 %outer_mixed.3 = bf16[4,4,104,768]{3,2,1,0:T(8,128)(2,1)} custom-call(s32[4]{0:T(128)} %pad_add_fusion.me_ref, bf16[512,2304]{1,0:T(8,128)(2,1)} %copy-done.10, bf16[512,768]{1,0:T(8,128)(2,1)} %copy-done.16, bf16[640,1536]{1,0:T(8,128)(2,1)} %copy-done.12, bf16[640,768]{1,0:T(8,128)(2,1)} %copy-done.15, bf16[512,768]{1,0:T(8,128)(2,1)} %get-tuple-element.118.att_ref, ...), custom_call_target="tpu_custom_call" | custom-call | tf_op jit(solution)/shard_map/outer_mixed/pallas_call | solution.py:392
  264.5 7.4 %outer_mixed.2 = bf16[4,4,104,768]{3,2,1,0:T(8,128)(2,1)} custom-call(s32[4]{0:T(128)} %pad_add_fusion.me_ref, bf16[512,2304]{1,0:T(8,128)(2,1)} %copy-done.10, bf16[512,768]{1,0:T(8,128)(2,1)} %copy-done.16, bf16[640,1536]{1,0:T(8,128)(2,1)} %copy-done.12, bf16[640,768]{1,0:T(8,128)(2,1)} %copy-done.15, bf16[512,768]{1,0:T(8,128)(2,1)} %get-tuple-element.118.att_ref, ...), custom_call_target="tpu_custom_call" | custom-call | tf_op jit(solution)/shard_map/outer_mixed/pallas_call | solution.py:392
  273.7 7.8 %collective-permute-done.17 = bf16[1,96,768]{2,1,0:T(8,128)(2,1)S(1)} collective-permute-done((bf16[1,96,768]{2,1,0:T(8,128)(2,1)}, bf16[1,96,768]{2,1,0:T(8,128)(2,1)S(1)}, u32[]{:S(2)}, u32[]{:S(2)}) %collective-permute-start.17) | collective-permute-done | bytes 147488 | tf_op jit(solution)/shard_map/ppermute | solution.py:520
  285.0 15.2 %collective-permute-done.18 = bf16[8,104,768]{2,1,0:T(8,128)(2,1)S(1)} collective-permute-done((bf16[8,104,768]{2,1,0:T(8,128)(2,1)S(1)}, bf16[8,104,768]{2,1,0:T(8,128)(2,1)S(1)}, u32[]{:S(2)}, u32[]{:S(2)}) %collective-permute-start.18) | collective-permute-done | bytes 1277984 | tf_op jit(solution)/shard_map/ppermute | solution.py:520
  301.6 12.1 %collective-permute-done.20 = bf16[2,96,768]{2,1,0:T(8,128)(2,1)S(1)} collective-permute-done((bf16[2,96,768]{2,1,0:T(8,128)(2,1)S(1)}, bf16[2,96,768]{2,1,0:T(8,128)(2,1)S(1)}, u32[]{:S(2)}, u32[]{:S(2)}) %collective-permute-start.20) | collective-permute-done | bytes 294944 | tf_op jit(solution)/shard_map/ppermute | solution.py:520
  314.1 9.4 %collective-permute-done.22 = bf16[2,104,768]{2,1,0:T(8,128)(2,1)S(1)} collective-permute-done((bf16[2,104,768]{2,1,0:T(8,128)(2,1)S(1)}, bf16[2,104,768]{2,1,0:T(8,128)(2,1)S(1)}, u32[]{:S(2)}, u32[]{:S(2)}) %collective-permute-start.22) | collective-permute-done | bytes 319520 | tf_op jit(solution)/shard_map/ppermute | solution.py:520
  324.5 8.6 %collective-permute-done.23 = bf16[1,104,768]{2,1,0:T(8,128)(2,1)S(1)} collective-permute-done((bf16[1,104,768]{2,1,0:T(8,128)(2,1)S(1)}, bf16[1,104,768]{2,1,0:T(8,128)(2,1)S(1)}, u32[]{:S(2)}, u32[]{:S(2)}) %collective-permute-start.23) | collective-permute-done | bytes 159776 | tf_op jit(solution)/shard_map/ppermute | solution.py:520
  333.3 7.8 %collective-permute-done.24 = bf16[1,104,768]{2,1,0:T(8,128)(2,1)S(1)} collective-permute-done((bf16[1,104,768]{2,1,0:T(8,128)(2,1)S(1)}, bf16[1,104,768]{2,1,0:T(8,128)(2,1)S(1)}, u32[]{:S(2)}, u32[]{:S(2)}) %collective-permute-start.24) | collective-permute-done | bytes 159776 | tf_op jit(solution)/shard_map/ppermute | solution.py:520
  341.2 9.4 %collective-permute-done.25 = bf16[2,104,768]{2,1,0:T(8,128)(2,1)S(1)} collective-permute-done((bf16[2,104,768]{2,1,0:T(8,128)(2,1)S(1)}, bf16[2,104,768]{2,1,0:T(8,128)(2,1)S(1)}, u32[]{:S(2)}, u32[]{:S(2)}) %collective-permute-start.25) | collective-permute-done | bytes 319520 | tf_op jit(solution)/shard_map/ppermute | solution.py:520
  353.0 5.8 %collective-permute-done.29 = bf16[2,96,768]{2,1,0:T(8,128)(2,1)S(1)} collective-permute-done((bf16[2,96,768]{2,1,0:T(8,128)(2,1)S(1)}, bf16[2,96,768]{2,1,0:T(8,128)(2,1)S(1)}, u32[]{:S(2)}, u32[]{:S(2)}) %collective-permute-start.29) | collective-permute-done | bytes 294944 | tf_op jit(solution)/shard_map/ppermute | solution.py:520
  361.3 11.4 %collective-permute-done.33 = bf16[4,96,768]{2,1,0:T(8,128)(2,1)S(1)} collective-permute-done((bf16[4,96,768]{2,1,0:T(8,128)(2,1)S(1)}, bf16[4,96,768]{2,1,0:T(8,128)(2,1)S(1)}, u32[]{:S(2)}, u32[]{:S(2)}) %collective-permute-start.33) | collective-permute-done | bytes 589856 | tf_op jit(solution)/shard_map/ppermute | solution.py:520
  372.9 12.5 %collective-permute-done.30 = bf16[4,96,768]{2,1,0:T(8,128)(2,1)S(1)} collective-permute-done((bf16[4,96,768]{2,1,0:T(8,128)(2,1)S(1)}, bf16[4,96,768]{2,1,0:T(8,128)(2,1)S(1)}, u32[]{:S(2)}, u32[]{:S(2)}) %collective-permute-start.30) | collective-permute-done | bytes 589856 | tf_op jit(solution)/shard_map/ppermute | solution.py:520
  387.9 10.4 %collective-permute-done.34 = bf16[8,96,768]{2,1,0:T(8,128)(2,1)S(1)} collective-permute-done((bf16[8,96,768]{2,1,0:T(8,128)(2,1)S(1)}, bf16[8,96,768]{2,1,0:T(8,128)(2,1)S(1)}, u32[]{:S(2)}, u32[]{:S(2)}) %collective-permute-start.34) | collective-permute-done | bytes 1179680 | tf_op jit(solution)/shard_map/ppermute | solution.py:520
  400.5 10.4 %collective-permute-done.31 = bf16[8,96,768]{2,1,0:T(8,128)(2,1)S(1)} collective-permute-done((bf16[8,96,768]{2,1,0:T(8,128)(2,1)S(1)}, bf16[8,96,768]{2,1,0:T(8,128)(2,1)S(1)}, u32[]{:S(2)}, u32[]{:S(2)}) %collective-permute-start.31) | collective-permute-done | bytes 1179680 | tf_op jit(solution)/shard_map/ppermute | solution.py:520
  420.6 8.7 %spread.3 = f32[3072,768]{1,0:T(8,128)} custom-call(s32[4]{0:T(128)} %pad_add_fusion.me_ref, bf16[4,4,96,768]{3,2,1,0:T(8,128)(2,1)} %bitcast.51, bf16[4,4,96,768]{3,2,1,0:T(8,128)(2,1)} %bitcast.55), custom_call_target="tpu_custom_call" | custom-call | tf_op jit(solution)/shard_map/spread/pallas_call | solution.py:448
  429.3 9.1 %spread.2 = f32[768,3072]{1,0:T(8,128)} custom-call(s32[4]{0:T(128)} %pad_add_fusion.me_ref, bf16[4,4,96,768]{3,2,1,0:T(8,128)(2,1)} %bitcast.16.f_ref, bf16[4,4,96,768]{3,2,1,0:T(8,128)(2,1)} %bitcast.17.g_ref), custom_call_target="tpu_custom_call" | custom-call | tf_op jit(solution)/shard_map/spread/pallas_call | solution.py:448
  438.4 9.3 %mixed_spread.1 = (f32[768,2304]{1,0:T(8,128)}, f32[768,768]{1,0:T(8,128)}, f32[16,768]{1,0:T(8,128)}) custom-call(s32[4]{0:T(128)} %pad_add_fusion.me_ref, bf16[4,4,104,768]{3,2,1,0:T(8,128)(2,1)} %bitcast.50, bf16[4,4,104,768]{3,2,1,0:T(8,128)(2,1)} %bitcast.15.g_ref), custom_call_target="tpu_custom_call" | custom-call | tf_op jit(solution)/shard_map/mixed_spread/pallas_call | solution.py:484
  (277 shorter events, 136.8 us)
Async XLA Ops:
  0.7 23.2 %collective-permute-start = (bf16[512,768]{1,0:T(8,128)(2,1)}, bf16[512,768]{1,0:T(8,128)(2,1)}, u32[]{:S(2)}, u32[]{:S(2)}) collective-permute-start(bf16[512,768]{1,0:T(8,128)(2,1)} %param.18), channel_id=1, source_target_pairs={{0,2},{4,6},{8,10},{12,14},{16,18},{20,22},{24,26},{28,30}} | collective-permute-start | bytes 2359304 | tf_op jit(solution)/shard_map/ppermute | solution.py:642
  24.0 21.8 %collective-permute-start.1 = (bf16[512,768]{1,0:T(8,128)(2,1)S(1)}, bf16[512,768]{1,0:T(8,128)(2,1)}, u32[]{:S(2)}, u32[]{:S(2)}) collective-permute-start(bf16[512,768]{1,0:T(8,128)(2,1)S(1)} %broadcast_select_fusion.1), channel_id=1, source_target_pairs={{0,1},{2,3},{4,5},{6,7},{8,9},{10,11},{12,13},{14,15},{16,17},{18,... | collective-permute-start | bytes 2359304 | tf_op jit(solution)/shard_map/ppermute | solution.py:654
  26.9 18.9 %collective-permute-start.2 = (bf16[128,768]{1,0:T(8,128)(2,1)}, bf16[128,768]{1,0:T(8,128)(2,1)}, u32[]{:S(2)}, u32[]{:S(2)}) collective-permute-start(bf16[128,768]{1,0:T(8,128)(2,1)} %slice.193), channel_id=1, source_target_pairs={{0,1},{1,2},{2,3},{4,5},{5,6},{6,7},{8,9},{9,10},{10,11},{12,13},{... | collective-permute-start | bytes 589832 | tf_op jit(solution)/shard_map/ppermute | solution.py:637
  110.6 31.5 %collective-permute-start.5 = (bf16[16,96,768]{2,1,0:T(8,128)(2,1)}, bf16[16,96,768]{2,1,0:T(8,128)(2,1)}, u32[]{:S(2)}, u32[]{:S(2)}) collective-permute-start(bf16[16,96,768]{2,1,0:T(8,128)(2,1)} %bitcast.53), channel_id=1, source_target_pairs={{0,4},{4,0},{8,12},{12,8},{16,20},{20,16},{24,28},{28,24},{1,5},{5... | collective-permute-start | bytes 7077896 | tf_op jit(solution)/shard_map/ppermute | solution.py:520
  111.1 16.4 %collective-permute-start.4 = (bf16[8,96,768]{2,1,0:T(8,128)(2,1)}, bf16[8,96,768]{2,1,0:T(8,128)(2,1)S(1)}, u32[]{:S(2)}, u32[]{:S(2)}) collective-permute-start(bf16[8,96,768]{2,1,0:T(8,128)(2,1)} %get-tuple-element.129), channel_id=1, source_target_pairs={{0,8},{4,20},{8,0},{12,28},{16,24},{20,4},{24,16},{28,12},{1,9},{5... | collective-permute-start | bytes 3538952 | tf_op jit(solution)/shard_map/ppermute | solution.py:520
  129.8 10.2 %collective-permute-start.6 = (bf16[4,96,768]{2,1,0:T(8,128)(2,1)}, bf16[4,96,768]{2,1,0:T(8,128)(2,1)}, u32[]{:S(2)}, u32[]{:S(2)}) collective-permute-start(bf16[4,96,768]{2,1,0:T(8,128)(2,1)} %get-tuple-element.135), channel_id=1, source_target_pairs={{0,16},{4,12},{8,24},{12,4},{16,0},{20,28},{24,8},{28,20},{1,17},{... | collective-permute-start | bytes 1769480 | tf_op jit(solution)/shard_map/ppermute | solution.py:520
  152.0 29.7 %collective-permute-start.8 = (bf16[8,96,768]{2,1,0:T(8,128)(2,1)}, bf16[8,96,768]{2,1,0:T(8,128)(2,1)}, u32[]{:S(2)}, u32[]{:S(2)}) collective-permute-start(bf16[8,96,768]{2,1,0:T(8,128)(2,1)} %get-tuple-element.147), channel_id=1, source_target_pairs={{0,8},{4,20},{8,0},{12,28},{16,24},{20,4},{24,16},{28,12},{1,9},{5... | collective-permute-start | bytes 3538952 | tf_op jit(solution)/shard_map/ppermute | solution.py:520
  157.7 23.7 %collective-permute-start.7 = (bf16[2,96,768]{2,1,0:T(8,128)(2,1)}, bf16[2,96,768]{2,1,0:T(8,128)(2,1)S(1)}, u32[]{:S(2)}, u32[]{:S(2)}) collective-permute-start(bf16[2,96,768]{2,1,0:T(8,128)(2,1)} %get-tuple-element.145), channel_id=1, source_target_pairs={{0,1},{1,0},{2,3},{3,2},{4,5},{5,4},{6,7},{7,6},{8,9},{9,8},{10,11... | collective-permute-start | bytes 884744 | tf_op jit(solution)/shard_map/ppermute | solution.py:520
  192.6 9.9 %collective-permute-start.10 = (bf16[4,96,768]{2,1,0:T(8,128)(2,1)S(1)}, bf16[4,96,768]{2,1,0:T(8,128)(2,1)S(1)}, u32[]{:S(2)}, u32[]{:S(2)}) collective-permute-start(bf16[4,96,768]{2,1,0:T(8,128)(2,1)S(1)} %get-tuple-element.156), channel_id=1, source_target_pairs={{0,16},{4,12},{8,24},{12,4},{16,0},{20,28},{24,8},{28,20},{1,17},{... | collective-permute-start | bytes 1769480 | tf_op jit(solution)/shard_map/ppermute | solution.py:520
  202.8 18.0 %collective-permute-start.11 = (bf16[512,768]{1,0:T(8,128)(2,1)S(1)}, bf16[512,768]{1,0:T(8,128)(2,1)S(1)}, u32[]{:S(2)}, u32[]{:S(2)}) collective-permute-start(bf16[512,768]{1,0:T(8,128)(2,1)S(1)} %slice.346), channel_id=1, source_target_pairs={{1,0},{3,2},{5,4},{7,6},{9,8},{11,10},{13,12},{15,14},{17,16},{19,... | collective-permute-start | bytes 2359304 | tf_op jit(solution)/shard_map/ppermute | solution.py:585
  220.9 32.5 %collective-permute-start.12 = (bf16[512,768]{1,0:T(8,128)(2,1)S(1)}, bf16[512,768]{1,0:T(8,128)(2,1)S(1)}, u32[]{:S(2)}, u32[]{:S(2)}) collective-permute-start(bf16[512,768]{1,0:T(8,128)(2,1)S(1)} %fusion.41), channel_id=1, source_target_pairs={{2,0},{6,4},{10,8},{14,12},{18,16},{22,20},{26,24},{30,28}} | collective-permute-start | bytes 2359304 | tf_op jit(solution)/shard_map/ppermute | solution.py:586
  222.3 31.1 %collective-permute-start.13 = (bf16[128,768]{1,0:T(8,128)(2,1)S(1)}, bf16[128,768]{1,0:T(8,128)(2,1)S(1)}, u32[]{:S(2)}, u32[]{:S(2)}) collective-permute-start(bf16[128,768]{1,0:T(8,128)(2,1)S(1)} %slice.347), channel_id=1, source_target_pairs={{1,0},{2,1},{3,2},{5,4},{6,5},{7,6},{9,8},{10,9},{11,10},{13,12},{... | collective-permute-start | bytes 589832 | tf_op jit(solution)/shard_map/ppermute | solution.py:700
  223.7 26.0 %collective-permute-start.14 = (bf16[1,96,768]{2,1,0:T(8,128)(2,1)S(1)}, bf16[1,96,768]{2,1,0:T(8,128)(2,1)S(1)}, u32[]{:S(2)}, u32[]{:S(2)}) collective-permute-start(bf16[1,96,768]{2,1,0:T(8,128)(2,1)S(1)} %add_convert_fusion.21), channel_id=1, source_target_pairs={{0,2},{1,3},{2,0},{3,1},{4,6},{5,7},{6,4},{7,5},{8,10},{9,11},{10,... | collective-permute-start | bytes 442376 | tf_op jit(solution)/shard_map/ppermute | solution.py:520
  228.0 24.6 %collective-permute-start.15 = (bf16[2,96,768]{2,1,0:T(8,128)(2,1)S(1)}, bf16[2,96,768]{2,1,0:T(8,128)(2,1)S(1)}, u32[]{:S(2)}, u32[]{:S(2)}) collective-permute-start(bf16[2,96,768]{2,1,0:T(8,128)(2,1)S(1)} %get-tuple-element.162), channel_id=1, source_target_pairs={{0,1},{1,0},{2,3},{3,2},{4,5},{5,4},{6,7},{7,6},{8,9},{9,8},{10,11... | collective-permute-start | bytes 884744 | tf_op jit(solution)/shard_map/ppermute | solution.py:520
  264.5 17.1 %collective-permute-start.16 = (bf16[16,104,768]{2,1,0:T(8,128)(2,1)}, bf16[16,104,768]{2,1,0:T(8,128)(2,1)S(1)}, u32[]{:S(2)}, u32[]{:S(2)}) collective-permute-start(bf16[16,104,768]{2,1,0:T(8,128)(2,1)} %bitcast.52), channel_id=1, source_target_pairs={{0,4},{4,0},{8,12},{12,8},{16,20},{20,16},{24,28},{28,24},{1,5},{5... | collective-permute-start | bytes 7667720 | tf_op jit(solution)/shard_map/ppermute | solution.py:520
  271.9 9.6 %collective-permute-start.17 = (bf16[1,96,768]{2,1,0:T(8,128)(2,1)}, bf16[1,96,768]{2,1,0:T(8,128)(2,1)S(1)}, u32[]{:S(2)}, u32[]{:S(2)}) collective-permute-start(bf16[1,96,768]{2,1,0:T(8,128)(2,1)} %get-tuple-element.165), channel_id=1, source_target_pairs={{0,2},{1,3},{2,0},{3,1},{4,6},{5,7},{6,4},{7,5},{8,10},{9,11},{10,... | collective-permute-start | bytes 442376 | tf_op jit(solution)/shard_map/ppermute | solution.py:520
  282.4 17.9 %collective-permute-start.18 = (bf16[8,104,768]{2,1,0:T(8,128)(2,1)S(1)}, bf16[8,104,768]{2,1,0:T(8,128)(2,1)S(1)}, u32[]{:S(2)}, u32[]{:S(2)}) collective-permute-start(bf16[8,104,768]{2,1,0:T(8,128)(2,1)S(1)} %get-tuple-element.167), channel_id=1, source_target_pairs={{0,8},{4,20},{8,0},{12,28},{16,24},{20,4},{24,16},{28,12},{1,9},{5... | collective-permute-start | bytes 3833864 | tf_op jit(solution)/shard_map/ppermute | solution.py:520
  300.6 13.2 %collective-permute-start.19 = (bf16[4,104,768]{2,1,0:T(8,128)(2,1)S(1)}, bf16[4,104,768]{2,1,0:T(8,128)(2,1)S(1)}, u32[]{:S(2)}, u32[]{:S(2)}) collective-permute-start(bf16[4,104,768]{2,1,0:T(8,128)(2,1)S(1)} %get-tuple-element.169), channel_id=1, source_target_pairs={{0,16},{4,12},{8,24},{12,4},{16,0},{20,28},{24,8},{28,20},{1,17},{... | collective-permute-start | bytes 1916936 | tf_op jit(solution)/shard_map/ppermute | solution.py:520
  300.7 13.0 %collective-permute-start.20 = (bf16[2,96,768]{2,1,0:T(8,128)(2,1)S(1)}, bf16[2,96,768]{2,1,0:T(8,128)(2,1)S(1)}, u32[]{:S(2)}, u32[]{:S(2)}) collective-permute-start(bf16[2,96,768]{2,1,0:T(8,128)(2,1)S(1)} %copy-done.29), channel_id=1, source_target_pairs={{0,1},{1,0},{2,3},{3,2},{4,5},{5,4},{6,7},{7,6},{8,9},{9,8},{10,11... | collective-permute-start | bytes 884744 | tf_op jit(solution)/shard_map/ppermute | solution.py:520
  300.8 13.0 %collective-permute-start.21 = (bf16[1,96,768]{2,1,0:T(8,128)(2,1)S(1)}, bf16[1,96,768]{2,1,0:T(8,128)(2,1)S(1)}, u32[]{:S(2)}, u32[]{:S(2)}) collective-permute-start(bf16[1,96,768]{2,1,0:T(8,128)(2,1)S(1)} %add_convert_fusion.18), channel_id=1, source_target_pairs={{0,2},{1,3},{2,0},{3,1},{4,6},{5,7},{6,4},{7,5},{8,10},{9,11},{10,... | collective-permute-start | bytes 442376 | tf_op jit(solution)/shard_map/ppermute | solution.py:520
  314.0 9.5 %collective-permute-start.22 = (bf16[2,104,768]{2,1,0:T(8,128)(2,1)S(1)}, bf16[2,104,768]{2,1,0:T(8,128)(2,1)S(1)}, u32[]{:S(2)}, u32[]{:S(2)}) collective-permute-start(bf16[2,104,768]{2,1,0:T(8,128)(2,1)S(1)} %get-tuple-element.175), channel_id=1, source_target_pairs={{0,1},{1,0},{2,3},{3,2},{4,5},{5,4},{6,7},{7,6},{8,9},{9,8},{10,11... | collective-permute-start | bytes 958472 | tf_op jit(solution)/shard_map/ppermute | solution.py:520
  323.6 9.6 %collective-permute-start.23 = (bf16[1,104,768]{2,1,0:T(8,128)(2,1)S(1)}, bf16[1,104,768]{2,1,0:T(8,128)(2,1)S(1)}, u32[]{:S(2)}, u32[]{:S(2)}) collective-permute-start(bf16[1,104,768]{2,1,0:T(8,128)(2,1)S(1)} %get-tuple-element.177), channel_id=1, source_target_pairs={{0,2},{1,3},{2,0},{3,1},{4,6},{5,7},{6,4},{7,5},{8,10},{9,11},{10,... | collective-permute-start | bytes 479240 | tf_op jit(solution)/shard_map/ppermute | solution.py:520
  341.1 9.5 %collective-permute-start.25 = (bf16[2,104,768]{2,1,0:T(8,128)(2,1)S(1)}, bf16[2,104,768]{2,1,0:T(8,128)(2,1)S(1)}, u32[]{:S(2)}, u32[]{:S(2)}) collective-permute-start(bf16[2,104,768]{2,1,0:T(8,128)(2,1)S(1)} %pad_maximum_fusion.10), channel_id=1, source_target_pairs={{0,1},{1,0},{2,3},{3,2},{4,5},{5,4},{6,7},{7,6},{8,9},{9,8},{10,11... | collective-permute-start | bytes 958472 | tf_op jit(solution)/shard_map/ppermute | solution.py:520
  350.7 10.5 %collective-permute-start.26 = (bf16[4,104,768]{2,1,0:T(8,128)(2,1)S(1)}, bf16[4,104,768]{2,1,0:T(8,128)(2,1)S(1)}, u32[]{:S(2)}, u32[]{:S(2)}) collective-permute-start(bf16[4,104,768]{2,1,0:T(8,128)(2,1)S(1)} %pad_maximum_fusion.7), channel_id=1, source_target_pairs={{0,16},{4,12},{8,24},{12,4},{16,0},{20,28},{24,8},{28,20},{1,17},{... | collective-permute-start | bytes 1916936 | tf_op jit(solution)/shard_map/ppermute | solution.py:520
  351.1 21.6 %collective-permute-start.33 = (bf16[4,96,768]{2,1,0:T(8,128)(2,1)S(1)}, bf16[4,96,768]{2,1,0:T(8,128)(2,1)S(1)}, u32[]{:S(2)}, u32[]{:S(2)}) collective-permute-start(bf16[4,96,768]{2,1,0:T(8,128)(2,1)S(1)} %pad_maximum_fusion.8), channel_id=1, source_target_pairs={{0,16},{4,12},{8,24},{12,4},{16,0},{20,28},{24,8},{28,20},{1,17},{... | collective-permute-start | bytes 1769480 | tf_op jit(solution)/shard_map/ppermute | solution.py:520
  358.9 26.4 %collective-permute-start.30 = (bf16[4,96,768]{2,1,0:T(8,128)(2,1)S(1)}, bf16[4,96,768]{2,1,0:T(8,128)(2,1)S(1)}, u32[]{:S(2)}, u32[]{:S(2)}) collective-permute-start(bf16[4,96,768]{2,1,0:T(8,128)(2,1)S(1)} %pad_maximum_fusion.9), channel_id=1, source_target_pairs={{0,16},{4,12},{8,24},{12,4},{16,0},{20,28},{24,8},{28,20},{1,17},{... | collective-permute-start | bytes 1769480 | tf_op jit(solution)/shard_map/ppermute | solution.py:520
  361.2 24.4 %collective-permute-start.27 = (bf16[8,104,768]{2,1,0:T(8,128)(2,1)S(1)}, bf16[8,104,768]{2,1,0:T(8,128)(2,1)S(1)}, u32[]{:S(2)}, u32[]{:S(2)}) collective-permute-start(bf16[8,104,768]{2,1,0:T(8,128)(2,1)S(1)} %pad_maximum_fusion.3), channel_id=1, source_target_pairs={{0,8},{4,20},{8,0},{12,28},{16,24},{20,4},{24,16},{28,12},{1,9},{5... | collective-permute-start | bytes 3833864 | tf_op jit(solution)/shard_map/ppermute | solution.py:520
  372.8 25.5 %collective-permute-start.34 = (bf16[8,96,768]{2,1,0:T(8,128)(2,1)S(1)}, bf16[8,96,768]{2,1,0:T(8,128)(2,1)S(1)}, u32[]{:S(2)}, u32[]{:S(2)}) collective-permute-start(bf16[8,96,768]{2,1,0:T(8,128)(2,1)S(1)} %pad_maximum_fusion.5), channel_id=1, source_target_pairs={{0,8},{4,20},{8,0},{12,28},{16,24},{20,4},{24,16},{28,12},{1,9},{5... | collective-permute-start | bytes 3538952 | tf_op jit(solution)/shard_map/ppermute | solution.py:520
  385.5 25.5 %collective-permute-start.31 = (bf16[8,96,768]{2,1,0:T(8,128)(2,1)S(1)}, bf16[8,96,768]{2,1,0:T(8,128)(2,1)S(1)}, u32[]{:S(2)}, u32[]{:S(2)}) collective-permute-start(bf16[8,96,768]{2,1,0:T(8,128)(2,1)S(1)} %pad_maximum_fusion.4), channel_id=1, source_target_pairs={{0,8},{4,20},{8,0},{12,28},{16,24},{20,4},{24,16},{28,12},{1,9},{5... | collective-permute-start | bytes 3538952 | tf_op jit(solution)/shard_map/ppermute | solution.py:520
  385.9 52.5 %collective-permute-start.28 = (bf16[16,104,768]{2,1,0:T(8,128)(2,1)S(1)}, bf16[16,104,768]{2,1,0:T(8,128)(2,1)}, u32[]{:S(2)}, u32[]{:S(2)}) collective-permute-start(bf16[16,104,768]{2,1,0:T(8,128)(2,1)S(1)} %pad_maximum_fusion), channel_id=1, source_target_pairs={{0,4},{4,0},{8,12},{12,8},{16,20},{20,16},{24,28},{28,24},{1,5},{5... | collective-permute-start | bytes 7667720 | tf_op jit(solution)/shard_map/ppermute | solution.py:520
  398.5 20.7 %collective-permute-start.35 = (bf16[16,96,768]{2,1,0:T(8,128)(2,1)S(1)}, bf16[16,96,768]{2,1,0:T(8,128)(2,1)S(1)}, u32[]{:S(2)}, u32[]{:S(2)}) collective-permute-start(bf16[16,96,768]{2,1,0:T(8,128)(2,1)S(1)} %pad_maximum_fusion.2), channel_id=1, source_target_pairs={{0,4},{4,0},{8,12},{12,8},{16,20},{20,16},{24,28},{28,24},{1,5},{5... | collective-permute-start | bytes 7077896 | tf_op jit(solution)/shard_map/ppermute | solution.py:520
  412.5 16.8 %collective-permute-start.32 = (bf16[16,96,768]{2,1,0:T(8,128)(2,1)}, bf16[16,96,768]{2,1,0:T(8,128)(2,1)}, u32[]{:S(2)}, u32[]{:S(2)}) collective-permute-start(bf16[16,96,768]{2,1,0:T(8,128)(2,1)} %pad_maximum_fusion.1), channel_id=1, source_target_pairs={{0,4},{4,0},{8,12},{12,8},{16,20},{20,16},{24,28},{28,24},{1,5},{5... | collective-permute-start | bytes 7077896 | tf_op jit(solution)/shard_map/ppermute | solution.py:520
  (64 other events, 653.6 us)
